TPU v7x, 256 devices: a whole 4x4x8 slice. The times are simulated.
256 devices in a mesh: lon: 32 (over y_hi, z, core), lat: 8 (over x, y_lo).
Axes of the slice: x: 4, y: 4 (y_hi: 2, y_lo: 2; y = y_hi * 2 + y_lo), z: 8, core: 2. Of those that a mesh axis runs over, the one named last changes fastest.
Arguments:
- inputs: bfloat16 [256, 1024, 192], P('lat', 'lon'), may hold values from -6 to 6
- cotangent: bfloat16 [256, 1024, 192], P('lat', 'lon'), may hold values from -6 to 6
- first_weight: bfloat16 [3, 3, 192, 192], replicated, may hold values from -0.15625 to 0.15625
- second_weight: bfloat16 [3, 3, 192, 192], replicated, may hold values from -0.15625 to 0.15625
Outputs:
- input_gradient: bfloat16 [256, 1024, 192], P('lat', 'lon')
- first_kernel_gradient: float32 [3, 3, 192, 192], replicated
- second_kernel_gradient: float32 [3, 3, 192, 192], replicated
All inputs are finite; a program needn't handle non-finite values.
Results may differ from a plain program's by a relative error of at most 0.0049.
Values may be sent and summed in bfloat16 or wider, within the bound.
A program may use at most 128 MiB of HBM per device.

v0:
```python
import math

import jax
import jax.numpy as jnp
from jax import lax
from jax.sharding import PartitionSpec as P

FIRST_SPREAD = 32
SECOND_SPREAD = 64


def with_halo(cells, sides, width):
    for axis, dim in sides:
        count = lax.axis_size(axis)
        ends = count - 1
        head = lax.slice_in_dim(cells, 0, width, axis=dim)
        tail = lax.slice_in_dim(cells, cells.shape[dim] - width, cells.shape[dim], axis=dim)
        cells = jnp.concatenate(
            [
                lax.ppermute(tail, axis, [(i, (i + 1) % count) for i in range(ends)]),
                cells,
                lax.ppermute(head, axis, [((i + 1) % count, i) for i in range(ends)]),
            ],
            axis=dim,
        )
    return cells


def from_behind(value, axis, steps):
    count = lax.axis_size(axis)
    pairs = [(source, (source + steps) % count) for source in range(count)]
    return lax.ppermute(value, axis, pairs)


def widened_field(field, dilation):
    rimmed = with_halo(field, (("lat", 0),), 1)
    border_width = field.shape[1]
    reach = -(-dilation // border_width)
    behind = []
    ahead_list = []
    for distance in range(reach, 0, -1):
        behind.append(from_behind(rimmed, "lon", distance))
    for distance in range(1, reach + 1):
        ahead_list.append(from_behind(rimmed, "lon", -distance))
    return (jnp.concatenate(behind + [rimmed] + ahead_list, axis=1), dilation)


def gather_taps(extended, offset, dilation, border_width):
    height = extended.shape[0] - 2
    pieces = []
    for row_off in range(3):
        for col_off in (-1, 0, 1):
            start = offset + col_off * dilation
            pieces.append(extended[row_off : row_off + height, start : start + border_width])
    return jnp.concatenate(pieces, axis=2).reshape(height * border_width, -1)


def flipped_kernel(weight):
    return jnp.transpose(weight[::-1, ::-1], (0, 1, 3, 2))


def contract_cells(stacked, other):
    return lax.dot_general(
        stacked, other, (((0,), (0,)), ((), ())), preferred_element_type=jnp.float32
    )


def shards(inputs, cotangent, first_weight, second_weight):
    height, border_width, channels = inputs.shape
    gradient_scale = 1.0 / math.sqrt(
        height * lax.axis_size("lat") * border_width * lax.axis_size("lon")
    )
    extended_input, input_shift = widened_field(inputs, FIRST_SPREAD)
    input_taps = gather_taps(extended_input, input_shift, FIRST_SPREAD, border_width)
    pre_activation = jnp.dot(
        input_taps, first_weight.reshape(-1, channels), preferred_element_type=jnp.float32
    )
    hidden_state = (
        jax.nn.silu(pre_activation).astype(jnp.bfloat16).reshape(height, border_width, channels)
    )
    extended_hidden, hidden_shift = widened_field(hidden_state, SECOND_SPREAD)
    hidden_taps = gather_taps(extended_hidden, hidden_shift, SECOND_SPREAD, border_width)
    extended_cotangent, cotangent_shift = widened_field(cotangent, SECOND_SPREAD)
    cotangent_taps = gather_taps(extended_cotangent, cotangent_shift, SECOND_SPREAD, border_width)
    hidden_gradient = jnp.dot(
        cotangent_taps,
        flipped_kernel(second_weight).reshape(-1, channels),
        preferred_element_type=jnp.float32,
    )
    part_two = contract_cells(hidden_taps, cotangent.reshape(-1, channels))
    sigma = jax.nn.sigmoid(pre_activation)
    pre_flat = (hidden_gradient * sigma * (1.0 + pre_activation * (1.0 - sigma))).astype(
        jnp.bfloat16
    )
    pre_activation_gradient = pre_flat.reshape(height, border_width, channels)
    extended_pre_gradient, pre_gradient_shift = widened_field(pre_activation_gradient, FIRST_SPREAD)
    pre_gradient_taps = gather_taps(
        extended_pre_gradient, pre_gradient_shift, FIRST_SPREAD, border_width
    )
    input_gradient = jnp.dot(
        pre_gradient_taps,
        flipped_kernel(first_weight).reshape(-1, channels),
        preferred_element_type=jnp.float32,
    )
    input_gradient = input_gradient.astype(jnp.bfloat16).reshape(height, border_width, channels)
    part_one = contract_cells(input_taps, pre_flat)
    summed_one, summed_two = lax.psum((part_one, part_two), ("lon", "lat"))
    first_kernel_gradient = (summed_one * gradient_scale).reshape(3, 3, channels, channels)
    second_kernel_gradient = (summed_two * gradient_scale).reshape(3, 3, channels, channels)
    return (input_gradient, first_kernel_gradient, second_kernel_gradient)


def solution(mesh):
    placed = (P("lat", "lon", None), P("lat", "lon", None), P(), P())
    return jax.shard_map(
        shards,
        mesh=mesh,
        in_specs=placed,
        out_specs=(P("lat", "lon", None), P(), P()),
        check_vma=False,
    )
```

profile of v0, /device:TPU:1, one launch (start us, length us, event | category | flops | bytes accessed | tf_op | source)
XLA Modules:
  0.0 405.4 jit_solution(7806731082396063454)
XLA Ops:
  7.2 0.8 fusion.10
  8.0 4.0 collective-permute-start.4
  12.1 1.3 collective-permute-start.5
  13.4 0.7 fusion.11
  14.1 4.0 collective-permute-start
  18.1 1.3 collective-permute-start.1
  19.4 1.2 reverse_bitcast_fusion.1
  20.6 0.6 constant_dynamic-update-slice_fusion.5
  21.2 2.8 pad_maximum_fusion.6
  24.1 0.6 constant_dynamic-update-slice_fusion.3
  24.7 1.5 collective-permute-start.7
  26.3 1.4 copy.22
  27.6 1.4 copy.36
  29.0 1.5 collective-permute-start.6
  30.6 0.6 constant_dynamic-update-slice_fusion.2
  31.2 1.2 pad_maximum_fusion.8
  32.4 0.6 constant_dynamic-update-slice_fusion
  33.0 10.2 %collective-permute-start.3 = (bf16[34,32,192]{2,1,0:T(8,128)(2,1)}, bf16[34,32,192]{2,1,0:T(8,128)(2,1)S(1)}, u32[]{:S(2)}, u32[]{:S(2)}) collective-permute-start(bf16[34,32,192]{2,1,0:T(8,128)(2,1)} %constant_dynamic-update-slice_fusion), channel_id=1, source_target_pairs={{0,240},{8,248},{16,0},{24,8},{32,16},{40,24},{48,32},{56,40},{64,... | collective-permute-start | bytes 1253384 | tf_op jit(solution)/shard_map/ppermute | solution.py:32
  43.2 1.2 fusion.6
  44.5 1.2 fusion.7
  45.7 6.9 %concatenate.72 = bf16[32,32,1728]{2,1,0:T(8,128)(2,1)} concatenate(bf16[32,32,192]{2,1,0:T(8,128)(2,1)} %get-tuple-element.25, bf16[32,32,192]{2,1,0:T(8,128)(2,1)} %get-tuple-element.38, bf16[32,32,192]{2,1,0:T(8,128)(2,1)} %get-tuple-element.22, bf16[32,32,192]{2,1,0:T(8,128)(2,1)} %get-tuple-element.24, bf16[32,32,192]{2,1,0:T(8,128)(2,1)S(1)} %copy-done.3, ...), dimensions={2} | concatenate | bytes 7077888 | tf_op jit(solution)/shard_map/concatenate | solution.py:55
  53.1 1.0 fusion.8
  54.2 4.7 %multiply_convert_fusion = (bf16[1024,192]{0,1:T(8,128)(2,1)}, f32[1024,192]{0,1:T(8,128)}) fusion(bf16[1024,1728]{1,0:T(8,128)(2,1)} %bitcast.42, bf16[1728,192]{1,0:T(8,128)(2,1)} %bitcast.60), kind=kOutput, calls=%fused_computation.7 | convolution fusion | flops 680460288 | bytes 5382144 | tf_op jit(solution)/shard_map/dot_general | solution.py:75
  58.9 1.0 collective-permute-done.2
  59.9 1.2 fusion.9
  61.0 6.6 %concatenate.68 = bf16[32,32,1728]{2,1,0:T(8,128)(2,1)} concatenate(bf16[32,32,192]{2,1,0:T(8,128)(2,1)} %get-tuple-element.31, bf16[32,32,192]{2,1,0:T(8,128)(2,1)S(1)} %copy-done.5, bf16[32,32,192]{2,1,0:T(8,128)(2,1)} %get-tuple-element.28, bf16[32,32,192]{2,1,0:T(8,128)(2,1)} %get-tuple-element.30, bf16[32,32,192]{2,1,0:T(8,128)(2,1)S(1)} %copy-done, ...), dimensions={2} | concatenate | bytes 7077888 | tf_op jit(solution)/shard_map/concatenate | solution.py:55
  67.7 4.0 fusion.1
  71.8 4.2 %collective-permute-start.8 = (bf16[1,32,192]{1,2,0:T(8,128)(2,1)S(1)}, bf16[1,32,192]{1,2,0:T(8,128)(2,1)S(1)}, u32[]{:S(2)}, u32[]{:S(2)}) collective-permute-start(bf16[1,32,192]{1,2,0:T(8,128)(2,1)S(1)} %get-tuple-element.48), channel_id=1, source_target_pairs={{0,1},{1,2},{2,3},{3,4},{4,5},{5,6},{6,7},{8,9},{9,10},{10,11},{11... | collective-permute-start | bytes 36872 | tf_op jit(solution)/shard_map/ppermute | solution.py:20
  76.0 1.3 collective-permute-start.9
  77.6 5.5 %collective-permute-start.12 = (bf16[1,32,192]{1,2,0:T(8,128)(2,1)S(1)}, bf16[1,32,192]{1,2,0:T(8,128)(2,1)S(1)}, u32[]{:S(2)}, u32[]{:S(2)}) collective-permute-start(bf16[1,32,192]{1,2,0:T(8,128)(2,1)S(1)} %get-tuple-element.46), channel_id=1, source_target_pairs={{0,1},{1,2},{2,3},{3,4},{4,5},{5,6},{6,7},{8,9},{9,10},{10,11},{11... | collective-permute-start | bytes 36872 | tf_op jit(solution)/shard_map/ppermute | solution.py:20
  83.1 1.3 collective-permute-start.13
  84.6 1.0 pad_maximum_fusion
  85.6 4.0 fusion.12
  90.0 0.9 pad_maximum_fusion.1
  90.9 8.9 %collective-permute-start.15 = (bf16[34,32,192]{2,1,0:T(8,128)(2,1)}, bf16[34,32,192]{2,1,0:T(8,128)(2,1)S(1)}, u32[]{:S(2)}, u32[]{:S(2)}) collective-permute-start(bf16[34,32,192]{2,1,0:T(8,128)(2,1)} %pad_maximum_fusion.1), channel_id=1, source_target_pairs={{0,240},{8,248},{16,0},{24,8},{32,16},{40,24},{48,32},{56,40},{64,... | collective-permute-start | bytes 1253384 | tf_op jit(solution)/shard_map/ppermute | solution.py:32
  99.9 1.1 pad_maximum_fusion.4
  101.0 2.0 copy.29
  103.0 2.0 copy.34
  105.0 1.1 pad_maximum_fusion.2
  106.2 1.2 fusion.5
  107.3 2.1 copy.28
  109.4 1.9 collective-permute-done.15
  111.3 1.2 fusion.2
  112.5 2.6 collective-permute-done.14
  115.1 1.2 fusion.3
  116.3 6.9 %concatenate.88 = bf16[32,32,1728]{2,1,0:T(8,128)(2,1)} concatenate(bf16[32,32,192]{2,1,0:T(8,128)(2,1)} %get-tuple-element.13, bf16[32,32,192]{2,1,0:T(8,128)(2,1)} %get-tuple-element.33, bf16[32,32,192]{2,1,0:T(8,128)(2,1)} %get-tuple-element.10, bf16[32,32,192]{2,1,0:T(8,128)(2,1)} %get-tuple-element.12, bf16[32,32,192]{2,1,0:T(8,128)(2,1)S(1)} %bitcast.46, ...), dimensions={2} | concatenate | bytes 7077888 | tf_op jit(solution)/shard_map/concatenate | solution.py:55
  123.2 0.8 constant_dynamic-update-slice_fusion.14
  124.0 4.0 convolution_bitcast_fusion
  128.2 0.9 copy.30
  129.2 0.9 copy.31
  130.8 0.8 constant_dynamic-update-slice_fusion.13
  131.6 1.8 constant_dynamic-update-slice_fusion.12
  133.4 1.8 constant_dynamic-update-slice_fusion.11
  135.2 0.8 constant_dynamic-update-slice_fusion.10
  135.9 0.8 constant_dynamic-update-slice_fusion.9
  136.7 0.8 constant_dynamic-update-slice_fusion.8
  137.5 0.8 constant_dynamic-update-slice_fusion.7
  138.3 0.8 constant_dynamic-update-slice_fusion.6
  139.1 3.1 convolution_convert_fusion
  142.2 1.0 copy.37
  143.2 250.0 %all-reduce.3.cloned.1.call-done = (f32[1728,192]{0,1:T(8,128)}, f32[1728,192]{0,1:T(8,128)}) async-done(((f32[1728,192]{0,1:T(8,128)}, f32[1728,192]{0,1:T(8,128)}), (f32[1728,192]{0,1:T(8,128)}, f32[1728,192]{0,1:T(8,128)})) %all-reduce.3.cloned.1.call-update) | async-done | bytes 2654224 | tf_op jit(solution)/shard_map/psum | solution.py:107
  393.2 1.9 broadcast_multiply_fusion
  395.1 1.7 copy.38
  396.8 1.7 copy.44
  (60 shorter events, 2.4 us)
Async XLA Ops:
  7.2 386.0 %all-reduce.3.cloned.1.call-start = ((), (), s32[]{:S(2)}) async-start(), calls=%async_computation | async-start | bytes 5505024 | tf_op jit(solution)/shard_map/psum | solution.py:107
  7.2 19.0 %copy-start.11 = (bf16[3,3,192,192]{3,2,1,0:T(8,128)(2,1)S(1)}, bf16[3,3,192,192]{3,2,1,0:T(8,128)(2,1)}, u32[]{:S(2)}) copy-start(bf16[3,3,192,192]{3,2,1,0:T(8,128)(2,1)} %param.6) | copy-start | bytes 1990660
  8.0 12.6 %collective-permute-start.4 = (bf16[1,32,192]{2,1,0:T(8,128)(2,1)S(1)}, bf16[1,32,192]{2,1,0:T(8,128)(2,1)S(1)}, u32[]{:S(2)}, u32[]{:S(2)}) collective-permute-start(bf16[1,32,192]{2,1,0:T(8,128)(2,1)S(1)} %get-tuple-element.40), channel_id=1, source_target_pairs={{0,1},{1,2},{2,3},{3,4},{4,5},{5,6},{6,7},{8,9},{9,10},{10,11},{11... | collective-permute-start | bytes 36872 | tf_op jit(solution)/shard_map/ppermute | solution.py:20
  12.1 9.2 %collective-permute-start.5 = (bf16[1,32,192]{2,1,0:T(8,128)(2,1)S(1)}, bf16[1,32,192]{2,1,0:T(8,128)(2,1)S(1)}, u32[]{:S(2)}, u32[]{:S(2)}) collective-permute-start(bf16[1,32,192]{2,1,0:T(8,128)(2,1)S(1)} %get-tuple-element.39), channel_id=1, source_target_pairs={{1,0},{2,1},{3,2},{4,3},{5,4},{6,5},{7,6},{9,8},{10,9},{11,10},{12... | collective-permute-start | bytes 36872 | tf_op jit(solution)/shard_map/ppermute | solution.py:22
  14.1 16.5 %collective-permute-start = (bf16[1,32,192]{2,1,0:T(8,128)(2,1)S(1)}, bf16[1,32,192]{2,1,0:T(8,128)(2,1)S(1)}, u32[]{:S(2)}, u32[]{:S(2)}) collective-permute-start(bf16[1,32,192]{2,1,0:T(8,128)(2,1)S(1)} %get-tuple-element.45), channel_id=1, source_target_pairs={{0,1},{1,2},{2,3},{3,4},{4,5},{5,6},{6,7},{8,9},{9,10},{10,11},{11... | collective-permute-start | bytes 36872 | tf_op jit(solution)/shard_map/ppermute | solution.py:20
  18.1 13.1 %collective-permute-start.1 = (bf16[1,32,192]{2,1,0:T(8,128)(2,1)S(1)}, bf16[1,32,192]{2,1,0:T(8,128)(2,1)S(1)}, u32[]{:S(2)}, u32[]{:S(2)}) collective-permute-start(bf16[1,32,192]{2,1,0:T(8,128)(2,1)S(1)} %get-tuple-element.44), channel_id=1, source_target_pairs={{1,0},{2,1},{3,2},{4,3},{5,4},{6,5},{7,6},{9,8},{10,9},{11,10},{12... | collective-permute-start | bytes 36872 | tf_op jit(solution)/shard_map/ppermute | solution.py:22
  21.2 9.9 %copy-start = (bf16[32,32,192]{2,1,0:T(8,128)(2,1)S(1)}, bf16[32,32,192]{2,1,0:T(8,128)(2,1)}, u32[]{:S(2)}) copy-start(bf16[32,32,192]{2,1,0:T(8,128)(2,1)} %param.5) | copy-start | bytes 1179652
  24.7 18.6 %collective-permute-start.7 = (bf16[34,32,192]{2,1,0:T(8,128)(2,1)}, bf16[34,32,192]{2,1,0:T(8,128)(2,1)S(1)}, u32[]{:S(2)}, u32[]{:S(2)}) collective-permute-start(bf16[34,32,192]{2,1,0:T(8,128)(2,1)} %constant_dynamic-update-slice_fusion.3), channel_id=1, source_target_pairs={{0,248},{8,0},{16,8},{24,16},{32,24},{40,32},{48,40},{56,48},{64,5... | collective-permute-start | bytes 1253384 | tf_op jit(solution)/shard_map/ppermute | solution.py:32
  29.0 15.4 %collective-permute-start.6 = (bf16[34,32,192]{2,1,0:T(8,128)(2,1)}, bf16[34,32,192]{2,1,0:T(8,128)(2,1)S(1)}, u32[]{:S(2)}, u32[]{:S(2)}) collective-permute-start(bf16[34,32,192]{2,1,0:T(8,128)(2,1)} %constant_dynamic-update-slice_fusion.3), channel_id=1, source_target_pairs={{0,8},{8,16},{16,24},{24,32},{32,40},{40,48},{48,56},{56,64},{64,7... | collective-permute-start | bytes 1253384 | tf_op jit(solution)/shard_map/ppermute | solution.py:32
  32.4 13.3 %copy-start.3 = (bf16[32,32,192]{2,1,0:T(8,128)(2,1)S(1)}, bf16[32,32,192]{2,1,0:T(8,128)(2,1)}, u32[]{:S(2)}) copy-start(bf16[32,32,192]{2,1,0:T(8,128)(2,1)} %param.4) | copy-start | bytes 1179652
  33.0 20.1 %collective-permute-start.3 = (bf16[34,32,192]{2,1,0:T(8,128)(2,1)}, bf16[34,32,192]{2,1,0:T(8,128)(2,1)S(1)}, u32[]{:S(2)}, u32[]{:S(2)}) collective-permute-start(bf16[34,32,192]{2,1,0:T(8,128)(2,1)} %constant_dynamic-update-slice_fusion), channel_id=1, source_target_pairs={{0,240},{8,248},{16,0},{24,8},{32,16},{40,24},{48,32},{56,40},{64,... | collective-permute-start | bytes 1253384 | tf_op jit(solution)/shard_map/ppermute | solution.py:32
  43.2 16.6 %collective-permute-start.2 = (bf16[34,32,192]{2,1,0:T(8,128)(2,1)}, bf16[34,32,192]{2,1,0:T(8,128)(2,1)S(1)}, u32[]{:S(2)}, u32[]{:S(2)}) collective-permute-start(bf16[34,32,192]{2,1,0:T(8,128)(2,1)} %constant_dynamic-update-slice_fusion), channel_id=1, source_target_pairs={{0,16},{8,24},{16,32},{24,40},{32,48},{40,56},{48,64},{56,72},{64,... | collective-permute-start | bytes 1253384 | tf_op jit(solution)/shard_map/ppermute | solution.py:32
  54.2 6.9 %copy-start.5 = (bf16[32,32,192]{2,1,0:T(8,128)(2,1)S(1)}, bf16[32,32,192]{2,1,0:T(8,128)(2,1)}, u32[]{:S(2)}) copy-start(bf16[32,32,192]{2,1,0:T(8,128)(2,1)} %get-tuple-element.42) | copy-start | bytes 1179652
  67.7 9.7 %copy-start.13 = (bf16[1024,192]{0,1:T(8,128)(2,1)S(1)}, bf16[1024,192]{0,1:T(8,128)(2,1)}, u32[]{:S(2)}) copy-start(bf16[1024,192]{0,1:T(8,128)(2,1)} %get-tuple-element.50) | copy-start | bytes 1179652
  71.7 13.9 %copy-start.1 = (bf16[1024,192]{0,1:T(8,128)(2,1)}, bf16[1024,192]{0,1:T(8,128)(2,1)S(1)}, u32[]{:S(2)}) copy-start(bf16[1024,192]{0,1:T(8,128)(2,1)S(1)} %fusion.1) | copy-start | bytes 1179652
  71.8 12.7 %collective-permute-start.8 = (bf16[1,32,192]{1,2,0:T(8,128)(2,1)S(1)}, bf16[1,32,192]{1,2,0:T(8,128)(2,1)S(1)}, u32[]{:S(2)}, u32[]{:S(2)}) collective-permute-start(bf16[1,32,192]{1,2,0:T(8,128)(2,1)S(1)} %get-tuple-element.48), channel_id=1, source_target_pairs={{0,1},{1,2},{2,3},{3,4},{4,5},{5,6},{6,7},{8,9},{9,10},{10,11},{11... | collective-permute-start | bytes 36872 | tf_op jit(solution)/shard_map/ppermute | solution.py:20
  76.0 8.5 %collective-permute-start.9 = (bf16[1,32,192]{1,2,0:T(8,128)(2,1)S(1)}, bf16[1,32,192]{1,2,0:T(8,128)(2,1)S(1)}, u32[]{:S(2)}, u32[]{:S(2)}) collective-permute-start(bf16[1,32,192]{1,2,0:T(8,128)(2,1)S(1)} %get-tuple-element.49), channel_id=1, source_target_pairs={{1,0},{2,1},{3,2},{4,3},{5,4},{6,5},{7,6},{9,8},{10,9},{11,10},{12... | collective-permute-start | bytes 36872 | tf_op jit(solution)/shard_map/ppermute | solution.py:22
  77.6 12.2 %collective-permute-start.12 = (bf16[1,32,192]{1,2,0:T(8,128)(2,1)S(1)}, bf16[1,32,192]{1,2,0:T(8,128)(2,1)S(1)}, u32[]{:S(2)}, u32[]{:S(2)}) collective-permute-start(bf16[1,32,192]{1,2,0:T(8,128)(2,1)S(1)} %get-tuple-element.46), channel_id=1, source_target_pairs={{0,1},{1,2},{2,3},{3,4},{4,5},{5,6},{6,7},{8,9},{9,10},{10,11},{11... | collective-permute-start | bytes 36872 | tf_op jit(solution)/shard_map/ppermute | solution.py:20
  83.1 6.8 %collective-permute-start.13 = (bf16[1,32,192]{1,2,0:T(8,128)(2,1)S(1)}, bf16[1,32,192]{1,2,0:T(8,128)(2,1)S(1)}, u32[]{:S(2)}, u32[]{:S(2)}) collective-permute-start(bf16[1,32,192]{1,2,0:T(8,128)(2,1)S(1)} %get-tuple-element.47), channel_id=1, source_target_pairs={{1,0},{2,1},{3,2},{4,3},{5,4},{6,5},{7,6},{9,8},{10,9},{11,10},{12... | collective-permute-start | bytes 36872 | tf_op jit(solution)/shard_map/ppermute | solution.py:22
  85.6 20.5 %collective-permute-start.10 = (bf16[34,32,192]{2,1,0:T(8,128)(2,1)}, bf16[34,32,192]{2,1,0:T(8,128)(2,1)S(1)}, u32[]{:S(2)}, u32[]{:S(2)}) collective-permute-start(bf16[34,32,192]{2,1,0:T(8,128)(2,1)} %pad_maximum_fusion), channel_id=1, source_target_pairs={{0,8},{8,16},{16,24},{24,32},{32,40},{40,48},{48,56},{56,64},{64,7... | collective-permute-start | bytes 1253384 | tf_op jit(solution)/shard_map/ppermute | solution.py:32
  90.9 20.4 %collective-permute-start.15 = (bf16[34,32,192]{2,1,0:T(8,128)(2,1)}, bf16[34,32,192]{2,1,0:T(8,128)(2,1)S(1)}, u32[]{:S(2)}, u32[]{:S(2)}) collective-permute-start(bf16[34,32,192]{2,1,0:T(8,128)(2,1)} %pad_maximum_fusion.1), channel_id=1, source_target_pairs={{0,240},{8,248},{16,0},{24,8},{32,16},{40,24},{48,32},{56,40},{64,... | collective-permute-start | bytes 1253384 | tf_op jit(solution)/shard_map/ppermute | solution.py:32
  99.9 15.2 %collective-permute-start.14 = (bf16[34,32,192]{2,1,0:T(8,128)(2,1)}, bf16[34,32,192]{2,1,0:T(8,128)(2,1)S(1)}, u32[]{:S(2)}, u32[]{:S(2)}) collective-permute-start(bf16[34,32,192]{2,1,0:T(8,128)(2,1)} %pad_maximum_fusion.1), channel_id=1, source_target_pairs={{0,16},{8,24},{16,32},{24,40},{32,48},{40,56},{48,64},{56,72},{64,... | collective-permute-start | bytes 1253384 | tf_op jit(solution)/shard_map/ppermute | solution.py:32
  101.0 27.0 %collective-permute-start.11 = (bf16[34,32,192]{2,1,0:T(8,128)(2,1)}, bf16[34,32,192]{2,1,0:T(8,128)(2,1)S(1)}, u32[]{:S(2)}, u32[]{:S(2)}) collective-permute-start(bf16[34,32,192]{2,1,0:T(8,128)(2,1)} %pad_maximum_fusion), channel_id=1, source_target_pairs={{0,248},{8,0},{16,8},{24,16},{32,24},{40,32},{48,40},{56,48},{64,5... | collective-permute-start | bytes 1253384 | tf_op jit(solution)/shard_map/ppermute | solution.py:32
  107.3 9.0 %copy-start.4 = (bf16[32,32,192]{2,1,0:T(8,128)(2,1)S(1)}, bf16[32,32,192]{2,1,0:T(8,128)(2,1)}, u32[]{:S(2)}) copy-start(bf16[32,32,192]{2,1,0:T(8,128)(2,1)} %get-tuple-element.32) | copy-start | bytes 1179652
  116.3 6.9 %copy-start.10 = (bf16[1024,192]{0,1:T(8,128)(2,1)S(1)}, bf16[1024,192]{0,1:T(8,128)(2,1)}, u32[]{:S(2)}) copy-start(bf16[1024,192]{0,1:T(8,128)(2,1)} %copy.28) | copy-start | bytes 1179652
  128.0 1.2 copy-start.7
  128.0 2.3 copy-start.6
  128.2 2.5 copy-start.9
  130.3 4.8 %copy-start.2 = (bf16[1024,192]{0,1:T(8,128)(2,1)S(1)}, bf16[1024,192]{0,1:T(8,128)(2,1)}, u32[]{:S(2)}) copy-start(bf16[1024,192]{0,1:T(8,128)(2,1)} %copy-done.1) | copy-start | bytes 1179652
  130.7 6.8 %copy-start.8 = (bf16[1024,192]{0,1:T(8,128)(2,1)S(1)}, bf16[1024,192]{0,1:T(8,128)(2,1)}, u32[]{:S(2)}) copy-start(bf16[1024,192]{0,1:T(8,128)(2,1)} %copy.34) | copy-start | bytes 1179652
  130.8 8.3 %copy-start.12 = (bf16[3,3,192,192]{3,2,1,0:T(8,128)(2,1)S(1)}, bf16[3,3,192,192]{3,2,1,0:T(8,128)(2,1)}, u32[]{:S(2)}) copy-start(bf16[3,3,192,192]{3,2,1,0:T(8,128)(2,1)} %copy.36) | copy-start | bytes 1990660
Sparse Core Ops, SparseCore 0:
  130.9 262.2 all-reduce.2
where the time goes:
time: 408 us; the launch traced here: 405 us
  waiting for transfers between devices  256 us (63%)
  local copies, waits for them, and re-layouts  59.8 us (15%)
  starting transfers between devices  45.1 us (11%)
  matrix products  19.9 us (5%)
  between operations  14.3 us (4%)
  other arithmetic  10.2 us (2%)
    psum x1, waiting for transfers between devices, shards(): summed_one, summed_two = lax.psum((part_one, part_two), ('lon', 'lat'))  250 us
    concatenate x12, local copies, waits for them, and re-layouts, gather_taps(): return jnp.concatenate(pieces, axis=2).reshape(height * border_width, -1)  29.8 us
    ppermute x8, starting transfers between devices, from_behind(): return lax.ppermute(value, axis, pairs)  22.2 us
    ppermute x4, starting transfers between devices, with_halo(): lax.ppermute(tail, axis, [(i, (i + 1) % count) for i in range(ends)])  17.7 us
    unnamed x38, local copies, waits for them, and re-layouts  9.53 us
    slice x8, local copies, waits for them, and re-layouts, gather_taps(): extended[row_off:row_off + height, start:start + border_width]  8.44 us
    concatenate x6, other arithmetic, with_halo(): jnp.concatenate([lax.ppermute(tail, axis, [(i, (i + 1) % count) for i in...  8.29 us
  transfers between devices with their start and end apart: 17, of which 5 were waited for; matrix products, arithmetic and copies ran while one was open for 17% of the time, Pallas kernels for 0%

commit v1 on v0

v1 whole, which is shorter than its diff:
```python
import functools
import math

import jax
import jax.numpy as jnp
from jax import lax
from jax.experimental import pallas as pl
from jax.experimental.pallas import tpu as pltpu
from jax.sharding import PartitionSpec as P

MESH = pl.DeviceIdType.MESH
BF = jnp.bfloat16
F32 = jnp.float32
ROW = 32
CELLS = 1024
EXT = 1152
C = 192
CP = 256
BLK = 256
UNITS = 336
TAPU = 36


def pack(cells):
    half = cells.shape[0] // 2
    tail = jnp.concatenate([cells[:half, 128:C], cells[half:, 128:C]], axis=1)
    return cells[:, :128], tail


def unpack_into(ref, slot, start, packed):
    n = packed.shape[0] * 2 // 3
    tail = packed[n:]
    zero = jnp.zeros((n // 2, 64), packed.dtype)
    ref[slot, start:start + n, 0:128] = packed[:n]
    ref[slot, start:start + n // 2, 128:256] = jnp.concatenate([tail[:, :64], zero], axis=1)
    ref[slot, start + n // 2:start + n, 128:256] = jnp.concatenate([tail[:, 64:], zero], axis=1)


class Exchange:
    def __init__(self, bufs, dist, lon, lat, n_lon, n_lat):
        (self.slab, self.rows, self.slab_in, self.rows_in,
         self.send, self.recv, self.ext) = bufs
        self.lat, self.n_lat = lat, n_lat
        self.behind = lax.rem(lon + dist, n_lon)
        self.ahead = lax.rem(lon + n_lon - dist, n_lon)
        self.lon = lon

    def targets(self):
        return (self.behind, self.ahead, self.lon)

    def slab_copy(self, k):
        return pltpu.make_async_remote_copy(
            src_ref=self.slab, dst_ref=self.slab_in.at[k],
            send_sem=self.send.at[k], recv_sem=self.recv.at[k],
            device_id={"lon": self.targets()[k], "lat": self.lat}, device_id_type=MESH)

    def row_copy(self, k, side):
        s = 2 + 2 * k + side
        lat = jnp.minimum(self.lat + 1, self.n_lat - 1) if side == 0 else jnp.maximum(self.lat - 1, 0)
        return pltpu.make_async_remote_copy(
            src_ref=self.rows.at[side], dst_ref=self.rows_in.at[2 * k + side],
            send_sem=self.send.at[s], recv_sem=self.recv.at[s],
            device_id={"lon": self.targets()[k], "lat": lat}, device_id_type=MESH)

    def load(self, cells):
        main, tail = pack(cells)
        self.slab[0:CELLS] = main
        self.slab[CELLS:] = tail
        for side, part in ((0, cells[CELLS - ROW:]), (1, cells[:ROW])):
            main, tail = pack(part)
            self.rows[side, 0:ROW] = main
            self.rows[side, ROW:] = tail

    def start(self):
        for k in (0, 1):
            self.slab_copy(k).start()

    def start_rows(self):
        for k in range(3):
            @pl.when(self.lat < self.n_lat - 1)
            def _():
                self.row_copy(k, 0).start()

            @pl.when(self.lat > 0)
            def _():
                self.row_copy(k, 1).start()

    def place_own(self, cells):
        self.ext[1, ROW:ROW + CELLS, 0:128] = cells[:, :128]
        self.ext[1, ROW:ROW + CELLS, 128:256] = jnp.concatenate(
            [cells[:, 128:C], jnp.zeros((CELLS, 64), BF)], axis=1)

    def arrive_rows(self, k):
        slot = (0, 2, 1)[k]
        zero = jnp.zeros((ROW, CP), BF)
        for side, start, here in ((0, 0, self.lat > 0), (1, ROW + CELLS, self.lat < self.n_lat - 1)):
            @pl.when(here)
            def _():
                self.row_copy(k, side).wait_recv()
                unpack_into(self.ext, slot, start, self.rows_in[2 * k + side])

            @pl.when(jnp.logical_not(here))
            def _():
                self.ext[slot, start:start + ROW] = zero
        self.ext[slot, ROW * 2 + CELLS:] = jnp.zeros((EXT - 2 * ROW - CELLS, CP), BF)

    def arrive(self, k):
        slot = (0, 2)[k]
        self.slab_copy(k).wait_recv()
        unpack_into(self.ext, slot, ROW, self.slab_in[k])

    def drain(self):
        for k in (0, 1):
            self.slab_copy(k).wait_send()
        for k in range(3):
            @pl.when(self.lat < self.n_lat - 1)
            def _():
                self.row_copy(k, 0).wait_send()

            @pl.when(self.lat > 0)
            def _():
                self.row_copy(k, 1).wait_send()


def exchange_scratch():
    return [
        pltpu.VMEM((CELLS * 3 // 2, 128), BF),
        pltpu.VMEM((2, ROW * 3 // 2, 128), BF),
        pltpu.VMEM((2, CELLS * 3 // 2, 128), BF),
        pltpu.VMEM((6, ROW * 3 // 2, 128), BF),
        pltpu.SemaphoreType.DMA((8,)),
        pltpu.SemaphoreType.DMA((8,)),
        pltpu.VMEM((3, EXT, CP), BF),
    ]


def kernel(n_lon, n_lat, x_ref, c_ref, w1_ref, w2_ref, dx_ref, ff_ref, *scratch):
    xb, cb, pb = scratch[0:7], scratch[7:14], scratch[14:21]
    (w1n, w1t, w2t, acc_x, acc_c, hid_t, x_t, gz,
     part, pair_in, s0, r1, s1, r2, r3, pair_sem, ssem1, rsem1, ssem2, rsem2,
     ssem3, rsem3, ssem4, rsem4, ssem5, rsem5, pair_sem2, ff) = scratch[21:]
    lon, lat = lax.axis_index("lon"), lax.axis_index("lat")
    core = lax.rem(lon, 2)
    z = lax.rem(lon // 2, 8)
    y = (lon // 16) * 2 + lax.rem(lat, 2)
    x = lat // 2

    def at(xx, yy, zz):
        return {"lon": (yy // 2) * 16 + zz * 2 + core, "lat": xx * 2 + lax.rem(yy, 2)}

    def first(k):
        return at(lax.rem(x + k * (1 - core), 4), lax.rem(y + k * core, 4), z)

    def second(k):
        return at(lax.rem(x + k * core, 4), lax.rem(y + k * (1 - core), 4), z)

    def third(k):
        return at(x, y, lax.rem(z + k, 8))

    partner = {"lon": lon + 1 - 2 * core, "lat": lat}
    pos1 = x * (1 - core) + y * core
    pos2 = y * (1 - core) + x * core

    barrier = pltpu.get_barrier_semaphore()

    def greet(dev):
        pl.semaphore_signal(barrier, inc=1, device_id=dev, device_id_type=MESH)

    for dl in (-2, -1, 1, 2):
        greet({"lon": lax.rem(lon + n_lon + dl, n_lon), "lat": lat})
    for da, here in ((-1, lat > 0), (1, lat < n_lat - 1)):
        @pl.when(here)
        def _():
            for dl in (-2, -1, 0, 1, 2):
                greet({"lon": lax.rem(lon + n_lon + dl, n_lon), "lat": lat + da})
    for k in (1, 2, 3):
        greet(first(k))
        greet(second(k))
    for k in range(1, 8):
        greet(third(k))

    xe = Exchange(xb, 1, lon, lat, n_lon, n_lat)
    ce = Exchange(cb, 2, lon, lat, n_lon, n_lat)
    pe = Exchange(pb, 1, lon, lat, n_lon, n_lat)
    xcells, ccells = x_ref[...], c_ref[...]
    xe.load(xcells)
    ce.load(ccells)
    beside = jnp.where(lat > 0, 5, 0) + jnp.where(lat < n_lat - 1, 5, 0)
    pl.semaphore_wait(barrier, 4 + 6 + 7 + beside)
    xe.start()
    ce.start()
    xe.start_rows()
    ce.start_rows()

    w1n[...] = jnp.zeros_like(w1n)
    w1t[...] = jnp.zeros_like(w1t)
    w2t[...] = jnp.zeros_like(w2t)
    for b in range(3):
        for a in range(3):
            w1n[b, a * CP:a * CP + C, 0:C] = w1_ref[a * 3 + b]
            w1t[b, 0:C, a * CP:a * CP + C] = w1_ref[(2 - a) * 3 + 2 - b]
            w2t[b, 0:C, a * CP:a * CP + C] = w2_ref[(2 - a) * 3 + 2 - b]
    gz[0:2 * ROW] = jnp.zeros((2 * ROW, CP), BF)
    gz[2 * ROW + CELLS:] = jnp.zeros((gz.shape[0] - 2 * ROW - CELLS, CP), BF)
    xe.place_own(xcells)
    ce.place_own(ccells)

    def taps(ext, slot, i):
        start = pl.multiple_of(i * BLK, BLK)
        return jnp.concatenate([ext[slot, pl.ds(start + a * ROW, BLK), :] for a in range(3)], axis=1)

    def straight(ext, slot, i, w):
        return jnp.dot(taps(ext, slot, i), w[slot], preferred_element_type=F32)

    def flipped(ext, slot, i, w):
        return lax.dot_general(taps(ext, slot, i), w[slot], (((1,), (1,)), ((), ())),
                               preferred_element_type=F32)

    def rows_of(i):
        return pl.ds(pl.multiple_of(i * BLK, BLK), BLK)

    def add_slab(acc, conv, ext, slot, w, new):
        @pl.loop(0, CELLS // BLK)
        def _(i):
            value = conv(ext, slot, i, w)
            acc[rows_of(i)] = value if new else acc[rows_of(i)] + value

    def put_tap(which, tap, grad):
        main = grad[:, :128].reshape(24, 8, 128)
        tail = jnp.concatenate([grad[:96, 128:C], grad[96:, 128:C]], axis=1).reshape(12, 8, 128)
        part[which, pl.ds(tap * TAPU, 24)] = main.astype(BF)
        part[which, pl.ds(tap * TAPU + 24, 12)] = tail.astype(BF)

    xe.arrive_rows(2)
    add_slab(acc_x, straight, xe.ext, 1, w1n, True)
    ce.arrive_rows(2)
    add_slab(acc_c, flipped, ce.ext, 1, w2t, True)
    x_t[1] = xe.ext[1].T
    for k, slot in ((0, 0), (1, 2)):
        xe.arrive_rows(k)
        xe.arrive(k)
        add_slab(acc_x, straight, xe.ext, slot, w1n, False)
        x_t[slot] = xe.ext[slot].T

    @pl.loop(0, CELLS // BLK)
    def _(i):
        pre = acc_x[rows_of(i)]
        sig = 1.0 / (1.0 + jnp.exp(-pre))
        hid_t[:, rows_of(i)] = (pre * sig).astype(BF).T
        acc_x[rows_of(i)] = sig * (1.0 + pre * (1.0 - sig))

    def second_grad(slot):
        @pl.loop(0, 3)
        def _(a):
            rhs = ce.ext[slot, pl.ds(pl.multiple_of((2 - a) * ROW, ROW), CELLS), :]
            put_tap(1, a * 3 + 2 - slot, jnp.dot(hid_t[0:C], rhs, preferred_element_type=F32))

    second_grad(1)
    for k, slot in ((0, 0), (1, 2)):
        ce.arrive_rows(k)
        ce.arrive(k)
        add_slab(acc_c, flipped, ce.ext, slot, w2t, False)
        second_grad(slot)

    @pl.loop(0, CELLS // BLK)
    def _(i):
        gz[pl.ds(pl.multiple_of(i * BLK + 2 * ROW, 2 * ROW), BLK)] = (
            acc_c[rows_of(i)] * acc_x[rows_of(i)]).astype(BF)
    pcells = gz[2 * ROW:2 * ROW + CELLS]
    pe.load(pcells[:, :C])
    pe.start()
    pe.start_rows()

    @pl.loop(0, 3)
    def _(a):
        rhs = gz[pl.ds(pl.multiple_of((2 - a) * ROW, ROW), EXT), :]
        for b in range(3):
            put_tap(0, a * 3 + b, jnp.dot(x_t[b, 0:C], rhs, preferred_element_type=F32))
    part[0, 324:] = jnp.zeros((UNITS - 324, 8, 128), BF)
    part[1, 324:] = jnp.zeros((UNITS - 324, 8, 128), BF)

    def remote(src, dst, ss, rs, dev):
        return pltpu.make_async_remote_copy(src_ref=src, dst_ref=dst, send_sem=ss, recv_sem=rs,
                                            device_id=dev, device_id_type=MESH)

    swap = remote(part.at[1 - core], pair_in, pair_sem.at[0], pair_sem.at[1], partner)
    swap.start()
    pe.place_own(pcells[:, :C])
    pe.arrive_rows(2)
    add_slab(acc_x, flipped, pe.ext, 1, w1t, True)
    swap.wait()
    s0[...] = (part[core].astype(F32) + pair_in[...].astype(F32)).astype(BF)
    QUART, SIX = UNITS // 4, UNITS // 16

    def chunk(ref, pos, size):
        return ref.at[pl.ds(pos * size, size)]

    def one(k):
        return remote(chunk(s0, lax.rem(pos1 + k, 4), QUART), r1.at[k - 1],
                      ssem1.at[k - 1], rsem1.at[k - 1], first(k))

    def two(k):
        return remote(chunk(s1, lax.rem(pos2 + k, 4), SIX), r2.at[k - 1],
                      ssem2.at[k - 1], rsem2.at[k - 1], second(k))

    def three(k):
        return remote(r3.at[z], r3.at[z], ssem3.at[k - 1], rsem3.at[k - 1], third(k))

    def three_in(k):
        spot = r3.at[lax.rem(z + 8 - k, 8)]
        return remote(spot, spot, ssem3.at[k - 1], rsem3.at[k - 1], third(k))

    def own(pos, size):
        return ff.at[core, pl.ds(pos, size)]

    def four(k):
        spot = own(pos1 * QUART + pos2 * SIX, SIX)
        return remote(spot, spot, ssem4.at[k - 1], rsem4.at[k - 1], second(k))

    def four_in(k):
        spot = own(pos1 * QUART + lax.rem(pos2 + 4 - k, 4) * SIX, SIX)
        return remote(spot, spot, ssem4.at[k - 1], rsem4.at[k - 1], second(k))

    def five(k):
        spot = own(pos1 * QUART, QUART)
        return remote(spot, spot, ssem5.at[k - 1], rsem5.at[k - 1], first(k))

    def five_in(k):
        spot = own(lax.rem(pos1 + 4 - k, 4) * QUART, QUART)
        return remote(spot, spot, ssem5.at[k - 1], rsem5.at[k - 1], first(k))

    for k in (1, 2, 3):
        one(k).start()
    pe.arrive_rows(0)
    pe.arrive(0)
    add_slab(acc_x, flipped, pe.ext, 0, w1t, False)
    for k in (1, 2, 3):
        one(k).wait()
    total = s0[pl.ds(pos1 * QUART, QUART)].astype(F32)
    for k in range(3):
        total += r1[k].astype(F32)
    s1[...] = total.astype(BF)
    for k in (1, 2, 3):
        two(k).start()
    pe.arrive_rows(1)
    pe.arrive(1)

    @pl.loop(0, CELLS // BLK)
    def _(i):
        value = acc_x[rows_of(i)] + flipped(pe.ext, 2, i, w1t)
        dx_ref[rows_of(i)] = value[:, :C].astype(BF)
    for k in (1, 2, 3):
        two(k).wait()
    total = s1[pl.ds(pos2 * SIX, SIX)].astype(F32)
    for k in range(3):
        total += r2[k].astype(F32)
    r3[z] = total.astype(BF)
    for k in range(1, 8):
        three(k).start()
    for k in range(1, 8):
        three(k).wait_send()
        three_in(k).wait_recv()
    total = r3[0].astype(F32)
    for k in range(1, 8):
        total += r3[k].astype(F32)
    ff[core, pl.ds(pos1 * QUART + pos2 * SIX, SIX)] = total.astype(BF)
    for k in (1, 2, 3):
        four(k).start()
    for k in (1, 2, 3):
        four(k).wait_send()
        four_in(k).wait_recv()
    for k in (1, 2, 3):
        five(k).start()
    for k in (1, 2, 3):
        five(k).wait_send()
        five_in(k).wait_recv()
    back = remote(ff.at[core], ff.at[core], pair_sem2.at[0], pair_sem2.at[1], partner)
    back.start()
    xe.drain()
    ce.drain()
    pe.drain()
    back.wait_send()
    remote(ff.at[1 - core], ff.at[1 - core], pair_sem2.at[0], pair_sem2.at[1], partner).wait_recv()
    ff_ref[...] = ff[...]


def finish(scale, ff_ref, g1_ref, g2_ref):
    for which, out in ((0, g1_ref), (1, g2_ref)):
        @pl.loop(0, 9)
        def _(t):
            main = ff_ref[which, pl.ds(t * TAPU, 24)].astype(F32).reshape(C, 128) * scale
            tail = ff_ref[which, pl.ds(t * TAPU + 24, 12)].astype(F32).reshape(96, 128) * scale
            row = pl.multiple_of(t * C, C)
            out[pl.ds(row, C), 0:128] = main
            out[pl.ds(row, 96), 128:C] = tail[:, :64]
            out[pl.ds(row + 96, 96), 128:C] = tail[:, 64:]


def shards(n_lon, n_lat, inputs, cotangent, first_weight, second_weight):
    height, width, channels = inputs.shape
    scale = 1.0 / math.sqrt(height * n_lat * width * n_lon)
    vmem = pl.BlockSpec(memory_space=pltpu.VMEM)
    quarter, six = UNITS // 4, UNITS // 16
    dma = pltpu.SemaphoreType.DMA
    scratch = exchange_scratch() * 3 + [
        pltpu.VMEM((3, 3 * CP, CP), BF),
        pltpu.VMEM((3, CP, 3 * CP), BF),
        pltpu.VMEM((3, CP, 3 * CP), BF),
        pltpu.VMEM((CELLS, CP), F32),
        pltpu.VMEM((CELLS, CP), F32),
        pltpu.VMEM((CP, CELLS), BF),
        pltpu.VMEM((3, CP, EXT), BF),
        pltpu.VMEM((EXT + 2 * ROW, CP), BF),
        pltpu.VMEM((2, UNITS, 8, 128), BF),
        pltpu.VMEM((UNITS, 8, 128), BF),
        pltpu.VMEM((UNITS, 8, 128), BF),
        pltpu.VMEM((3, quarter, 8, 128), BF),
        pltpu.VMEM((quarter, 8, 128), BF),
        pltpu.VMEM((3, six, 8, 128), BF),
        pltpu.VMEM((8, six, 8, 128), BF),
        dma((2,)), dma((3,)), dma((3,)), dma((3,)), dma((3,)),
        dma((7,)), dma((7,)), dma((3,)), dma((3,)), dma((3,)), dma((3,)), dma((2,)),
        pltpu.VMEM((2, UNITS, 8, 128), BF),
    ]
    dx, ff = pl.pallas_call(
        functools.partial(kernel, n_lon, n_lat),
        out_shape=(jax.ShapeDtypeStruct((CELLS, C), BF),
                   jax.ShapeDtypeStruct((2, UNITS, 8, 128), BF)),
        in_specs=[vmem] * 4,
        out_specs=(vmem, vmem),
        scratch_shapes=scratch,
        compiler_params=pltpu.CompilerParams(collective_id=0, has_side_effects=True,
                                             vmem_limit_bytes=56 << 20),
        name="conv_grads",
    )(inputs.reshape(CELLS, C), cotangent.reshape(CELLS, C),
      first_weight.reshape(9, C, C), second_weight.reshape(9, C, C))
    g1, g2 = pl.pallas_call(
        functools.partial(finish, scale),
        out_shape=(jax.ShapeDtypeStruct((9 * C, C), F32),) * 2,
        in_specs=[vmem],
        out_specs=(vmem, vmem),
        name="unpack_grads",
    )(ff)
    return (dx.reshape(height, width, channels), g1.reshape(3, 3, C, C), g2.reshape(3, 3, C, C))


def solution(mesh):
    placed = (P("lat", "lon", None), P("lat", "lon", None), P(), P())
    return jax.shard_map(
        functools.partial(shards, mesh.shape["lon"], mesh.shape["lat"]),
        mesh=mesh,
        in_specs=placed,
        out_specs=(P("lat", "lon", None), P(), P()),
        check_vma=False,
    )
```

time: 408 us -> 86.3 us (0.21)
  waiting for transfers between devices: 256 us -> 0 us
  Pallas kernels: 0 us -> 83.6 us
  local copies, waits for them, and re-layouts: 59.8 us -> 1.87 us
  starting transfers between devices: 45.1 us -> 0 us
  matrix products: 19.9 us -> 0 us
  between operations: 14.3 us -> 0.64 us
  other arithmetic: 10.2 us -> 0 us
    psum x1 -> x0, waiting for transfers between devices: 250 us -> none  [shards(): summed_one, summed_two = lax.psum((part_one, part_two), ('lon', 'lat'))]
    pallas_call x0 -> x2, Pallas kernels: none -> 83.6 us  [the longest x1 78.9 us: shards(): pl.pallas_call(functools.partial(kernel, n_lon, n_lat), out_shape=(jax.Sh...]
    ppermute x16 -> x0, starting transfers between devices: 45.1 us -> none  [the longest x8 22.2 us: from_behind(): return lax.ppermute(value, axis, pairs)]
    concatenate x14 -> x0, local copies, waits for them, and re-layouts: 31 us -> none  [the longest x12 29.8 us: gather_taps(): return jnp.concatenate(pieces, axis=2).reshape(height * border_width, -1)]
    dot_general x5 -> x0, matrix products: 19.9 us -> none  [the longest x2 8.04 us: contract_cells(): lax.dot_general(stacked, other, (((0,), (0,)), ((), ())), preferred_eleme...]
    slice x12 -> x0, local copies, waits for them, and re-layouts: 10.2 us -> none  [the longest x8 8.44 us: gather_taps(): extended[row_off:row_off + height, start:start + border_width]]
    concatenate x6 -> x0, other arithmetic: 8.29 us -> none  [with_halo(): jnp.concatenate([lax.ppermute(tail, axis, [(i, (i + 1) % count) for i in...]
    unnamed x38 -> x1, local copies, waits for them, and re-layouts: 9.53 us -> 1.87 us
  transfers between devices with their start and end apart: 17 -> 0, of which waited for: 5 -> 0; matrix products, arithmetic and copies ran while one was open for 17% -> 0% of each run, Pallas kernels for 0% -> 0%
where the time goes in v1:
time: 86.3 us; the launch traced here: 86.1 us
  Pallas kernels  83.6 us (97%)
  local copies, waits for them, and re-layouts  1.87 us (2%)
    pallas_call x1, Pallas kernels, shards(): pl.pallas_call(functools.partial(kernel, n_lon, n_lat), out_shape=(jax.Sh...  78.9 us
    pallas_call x1, Pallas kernels, shards(): pl.pallas_call(functools.partial(finish, scale), out_shape=(jax.ShapeDtyp...  4.62 us
    unnamed x1, local copies, waits for them, and re-layouts  1.87 us

profile of v1, /device:TPU:1, one launch (start us, length us, event | category | flops | bytes accessed | tf_op | source)
XLA Modules:
  0.0 86.1 jit_solution(1161657703288755780)
XLA Ops:
  0.6 78.9 %conv_grads.1 = (bf16[1024,192]{1,0:T(8,128)(2,1)}, bf16[2,336,8,128]{3,2,1,0:T(8,128)(2,1)}) custom-call(bf16[1024,192]{1,0:T(8,128)(2,1)} %bitcast.10, bf16[1024,192]{1,0:T(8,128)(2,1)} %bitcast.11, bf16[9,192,192]{2,1,0:T(8,128)(2,1)} %bitcast.7, bf16[9,192,192]{2,1,0:T(8,128)(2,1)} %bitcast.8), custom_call_target="tpu_custom_call" | custom-call | tf_op jit(solution)/shard_map/conv_grads/pallas_call | solution.py:425
  79.6 4.6 %unpack_grads.1 = (f32[1728,192]{1,0:T(8,128)}, f32[1728,192]{1,0:T(8,128)}) custom-call(bf16[2,336,8,128]{3,2,1,0:T(8,128)(2,1)} %get-tuple-element.8.ff_ref), custom_call_target="tpu_custom_call" | custom-call | tf_op jit(solution)/shard_map/unpack_grads/pallas_call | solution.py:437
  84.2 1.9 %copy.8 = bf16[32,32,192]{2,1,0:T(8,128)(2,1)} copy(bf16[32,32,192]{2,1,0:T(8,128)(2,1)} %bitcast.9) | data formatting | bytes 786432

commit v2 on v1

v2 whole, which is shorter than its diff:
```python
import functools
import math

import jax
import jax.numpy as jnp
from jax import lax
from jax.experimental import pallas as pl
from jax.experimental.pallas import tpu as pltpu
from jax.sharding import PartitionSpec as P

MESH = pl.DeviceIdType.MESH
BF = jnp.bfloat16
F32 = jnp.float32
ROW = 32
CELLS = 1024
EXT = 1152
C = 192
CP = 256
BLK = 512
UNITS = 352
TAPU = 36


def pack_tail(tail):
    half = tail.shape[0] // 2
    return jnp.concatenate([tail[:half], tail[half:]], axis=1)


def unpack_tail(ref, slot, start, packed):
    n = packed.shape[0]
    zero = jnp.zeros((n, 64), packed.dtype)
    ref[slot, start:start + n, 128:256] = jnp.concatenate([packed[:, :64], zero], axis=1)
    ref[slot, start + n:start + 2 * n, 128:256] = jnp.concatenate([packed[:, 64:], zero], axis=1)


class Exchange:
    def __init__(self, bufs, source, dist, lon, lat, n_lon, n_lat):
        (self.tail, self.rows, self.tail_in, self.rows_in,
         self.send, self.recv, self.ext) = bufs
        self.source = source
        self.lat, self.n_lat = lat, n_lat
        self.lon, self.dist, self.n_lon = lon, dist, n_lon

    def target(self, k):
        if isinstance(k, int) and k == 2:
            return self.lon
        return lax.rem(self.lon + self.n_lon + self.dist * (1 - 2 * k), self.n_lon)

    def crosses(self, k):
        place = lax.rem(self.lon, 16)
        return place >= 16 - self.dist if k == 0 else place < self.dist

    def comes_across(self, k):
        return self.crosses(1 - k)

    def copy(self, src, dst, s, lon, lat):
        return pltpu.make_async_remote_copy(
            src_ref=src, dst_ref=dst, send_sem=self.send.at[s], recv_sem=self.recv.at[s],
            device_id={"lon": lon, "lat": lat}, device_id_type=MESH)

    def main_copy(self, k):
        return self.copy(self.source, self.ext.at[2 * k, pl.ds(ROW, CELLS), pl.ds(0, 128)],
                         k, self.target(k), self.lat)

    def tail_copy(self, k):
        return self.copy(self.tail, self.tail_in.at[k], 2 + k, self.target(k), self.lat)

    def row_copy(self, k, side):
        lat = jnp.minimum(self.lat + 1, self.n_lat - 1) if side == 0 else jnp.maximum(self.lat - 1, 0)
        return self.copy(self.rows.at[side], self.rows_in.at[2 * k + side],
                         4 + 2 * k + side, self.target(k), lat)

    def start_slabs(self, across):
        for k in (0, 1):
            @pl.when(self.crosses(k) == across)
            def _():
                self.tail_copy(k).start()
                self.main_copy(k).start()

    def fill_rows(self, last, first):
        for side, part in ((0, last), (1, first)):
            self.rows[side, 0:ROW] = part[:, :128]
            self.rows[side, ROW:] = pack_tail(part[:, 128:C])

    def start_rows(self):
        for k in range(3):
            @pl.when(self.lat < self.n_lat - 1)
            def _():
                self.row_copy(k, 0).start()

            @pl.when(self.lat > 0)
            def _():
                self.row_copy(k, 1).start()

    def arrive_rows(self, k):
        slot = 1 if isinstance(k, int) and k == 2 else 2 * k
        zero = jnp.zeros((ROW, CP), BF)
        for side, start, here in ((0, 0, self.lat > 0), (1, ROW + CELLS, self.lat < self.n_lat - 1)):
            @pl.when(here)
            def _():
                self.row_copy(k, side).wait_recv()
                packed = self.rows_in[2 * k + side]
                self.ext[slot, start:start + ROW, 0:128] = packed[:ROW]
                unpack_tail(self.ext, slot, start, packed[ROW:])

            @pl.when(jnp.logical_not(here))
            def _():
                self.ext[slot, start:start + ROW] = zero

    def arrive(self, k):
        self.tail_copy(k).wait_recv()
        unpack_tail(self.ext, 2 * k, ROW, self.tail_in[k])
        self.main_copy(k).wait_recv()

    def drain(self):
        for k in (0, 1):
            self.main_copy(k).wait_send()
            self.tail_copy(k).wait_send()
        for k in range(3):
            @pl.when(self.lat < self.n_lat - 1)
            def _():
                self.row_copy(k, 0).wait_send()

            @pl.when(self.lat > 0)
            def _():
                self.row_copy(k, 1).wait_send()


def exchange_scratch():
    return [
        pltpu.VMEM((CELLS // 2, 128), BF),
        pltpu.VMEM((2, ROW * 3 // 2, 128), BF),
        pltpu.VMEM((2, CELLS // 2, 128), BF),
        pltpu.VMEM((6, ROW * 3 // 2, 128), BF),
        pltpu.SemaphoreType.DMA((10,)),
        pltpu.SemaphoreType.DMA((10,)),
        pltpu.VMEM((3, EXT, CP), BF),
    ]


HALF, QUART, SIXTH = UNITS // 2, UNITS // 8, UNITS // 32


def remote(src, dst, ss, rs, dev):
    return pltpu.make_async_remote_copy(src_ref=src, dst_ref=dst, send_sem=ss, recv_sem=rs,
                                        device_id=dev, device_id_type=MESH)


class Chain:
    def __init__(self, w, part, ff, refs, core, pos1, pos2, z, partner, first, second, third):
        self.w, self.part, self.ff = w, part, ff
        (self.pair_in, self.s0, self.own0, self.r1, self.s1, self.own1, self.r2, self.r3,
         self.pair, self.sem1, self.sem2, self.sem3, self.sem4, self.sem5,
         self.sem6, self.spare) = refs
        self.core, self.pos1, self.pos2, self.z = core, pos1, pos2, z
        self.partner, self.first, self.second, self.third = partner, first, second, third

    def swap(self):
        return remote(self.part.at[self.w, pl.ds((1 - self.core) * HALF, HALF)], self.pair_in,
                      self.pair.at[0], self.pair.at[1], self.partner)

    def to_first(self, k):
        spot = self.s0.at[pl.ds(lax.rem(self.pos1 + k, 4) * QUART, QUART)]
        return remote(spot, self.r1.at[k - 1], self.sem1.at[0, k - 1], self.sem1.at[1, k - 1], self.first(k))

    def to_second(self, k):
        spot = self.s1.at[pl.ds(lax.rem(self.pos2 + k, 4) * SIXTH, SIXTH)]
        return remote(spot, self.r2.at[k - 1], self.sem2.at[0, k - 1], self.sem2.at[1, k - 1], self.second(k))

    def to_third(self, k, back=0):
        spot = self.r3.at[lax.rem(self.z + back, 8)]
        return remote(spot, spot, self.sem3.at[0, k - 1], self.sem3.at[1, k - 1], self.third(k))

    def place(self, p1, p2, size):
        return self.ff.at[self.w, pl.ds(self.core * HALF + p1 * QUART + p2 * SIXTH, size)]

    def piece(self, k, back=0):
        spot = self.place(self.pos1, lax.rem(self.pos2 + back, 4), SIXTH)
        return remote(spot, spot, self.sem4.at[0, k - 1], self.sem4.at[1, k - 1], self.second(k))

    def spread(self, k, j, back=0):
        spot = self.place(lax.rem(self.pos1 + back, 4), lax.rem(self.pos2 + 4 - j, 4), SIXTH)
        return remote(spot, spot, self.sem5.at[0, k - 1, j], self.sem5.at[1, k - 1, j], self.first(k))

    def back(self, k, theirs=False):
        core = 1 - self.core if theirs else self.core
        spot = self.ff.at[self.w, pl.ds(core * HALF + lax.rem(self.pos1 + 4 - k, 4) * QUART, QUART)]
        return remote(spot, spot, self.sem6.at[0, k], self.sem6.at[1, k], self.partner)

    def swap_start(self):
        self.swap().start()

    def swap_end(self):
        self.swap().wait()
        mine = self.part[self.w, pl.ds(self.core * HALF, HALF)].astype(F32) + self.pair_in[...].astype(F32)
        self.s0[...] = mine.astype(BF)
        for k in (1, 2, 3):
            self.to_first(k).start()

    def first_end(self):
        spot = pl.ds(self.pos1 * QUART, QUART)
        total = (self.part[self.w, pl.ds(self.core * HALF + self.pos1 * QUART, QUART)].astype(F32)
                 + self.pair_in[spot].astype(F32))
        for k in (1, 2, 3):
            self.to_first(k).wait()
            total += self.r1[k - 1].astype(F32)
        self.own1[...] = total
        self.s1[...] = total.astype(BF)
        for k in (1, 2, 3):
            self.to_second(k).start()

    def second_end(self):
        total = self.own1[pl.ds(self.pos2 * SIXTH, SIXTH)]
        for k in (1, 2, 3):
            self.to_second(k).wait()
            total += self.r2[k - 1].astype(F32)
        self.r3[self.z] = total.astype(BF)
        for k in range(1, 8):
            self.to_third(k).start()

    def third_end(self):
        for k in range(1, 8):
            self.to_third(k).wait_send()
            self.to_third(k, 8 - k).wait_recv()
        total = self.r3[0].astype(F32)
        for k in range(1, 8):
            total += self.r3[k].astype(F32)
        self.ff[self.w, pl.ds(self.core * HALF + self.pos1 * QUART + self.pos2 * SIXTH, SIXTH)] = total.astype(BF)
        for k in (1, 2, 3):
            self.piece(k).start()
        for k in (1, 2, 3):
            self.spread(k, 0).start()

    def gather_second(self):
        for j in (1, 2, 3):
            self.piece(j, 4 - j).wait_recv()
            for k in (1, 2, 3):
                self.spread(k, j).start()
        self.back(0).start()

    def gather_first(self):
        for k in (1, 2, 3):
            for j in range(4):
                self.spread(k, j, 4 - k).wait_recv()
            self.back(k).start()

    def back_end(self):
        for k in range(4):
            self.back(k, True).wait_recv()
        for k in range(4):
            self.back(k).wait_send()
        for k in (1, 2, 3):
            self.piece(k).wait_send()
            for j in range(4):
                self.spread(k, j).wait_send()


def kernel(n_lon, n_lat, x_ref, c_ref, w1_ref, w2_ref, dx_ref, ff_ref, *scratch):
    xb, cb, pb = scratch[0:7], scratch[7:14], scratch[14:21]
    (xv, cv, wv1, wv2, load_sem, w1n, w1t, w2t, acc_x, acc_c, hid_t, x_t, gz, part, dxv, out_sem,
     ff) = scratch[21:38]
    chains = (scratch[38:54], scratch[54:70])
    lon, lat = lax.axis_index("lon"), lax.axis_index("lat")
    core = lax.rem(lon, 2)
    z = lax.rem(lon // 2, 8)
    y = (lon // 16) * 2 + lax.rem(lat, 2)
    x = lat // 2

    def at(xx, yy, zz):
        return {"lon": (yy // 2) * 16 + zz * 2 + core, "lat": xx * 2 + lax.rem(yy, 2)}

    def first(k):
        return at(lax.rem(x + k * (1 - core), 4), lax.rem(y + k * core, 4), z)

    def second(k):
        return at(lax.rem(x + k * core, 4), lax.rem(y + k * (1 - core), 4), z)

    def third(k):
        return at(x, y, lax.rem(z + k, 8))

    partner = {"lon": lon + 1 - 2 * core, "lat": lat}
    pos1 = x * (1 - core) + y * core
    pos2 = y * (1 - core) + x * core

    barrier = pltpu.get_barrier_semaphore()

    def greet(dev):
        pl.semaphore_signal(barrier, inc=1, device_id=dev, device_id_type=MESH)

    for dl in (-2, -1, 1, 2):
        greet({"lon": lax.rem(lon + n_lon + dl, n_lon), "lat": lat})
    for da, here in ((-1, lat > 0), (1, lat < n_lat - 1)):
        @pl.when(here)
        def _():
            for dl in (-2, -1, 0, 1, 2):
                greet({"lon": lax.rem(lon + n_lon + dl, n_lon), "lat": lat + da})
    for k in (1, 2, 3):
        greet(first(k))
        greet(second(k))
    for k in range(1, 8):
        greet(third(k))

    xe = Exchange(xb, x_ref.at[:, pl.ds(0, 128)], 1, lon, lat, n_lon, n_lat)
    ce = Exchange(cb, c_ref.at[:, pl.ds(0, 128)], 2, lon, lat, n_lon, n_lat)
    pe = Exchange(pb, gz.at[pl.ds(2 * ROW, CELLS), pl.ds(0, 128)], 1, lon, lat, n_lon, n_lat)
    loads = [pltpu.make_async_copy(src, dst, load_sem.at[i]) for i, (src, dst) in enumerate(
        ((x_ref, xv), (c_ref, cv), (w1_ref, wv1), (w2_ref, wv2)))]
    for load in loads:
        load.start()
    for e, v, load in ((xe, xv, loads[0]), (ce, cv, loads[1])):
        load.wait()
        e.fill_rows(v[CELLS - ROW:], v[:ROW])
    xe.tail[...] = pack_tail(xv[:, 128:C])
    beside = jnp.where(lat > 0, 5, 0) + jnp.where(lat < n_lat - 1, 5, 0)
    pl.semaphore_wait(barrier, 4 + 6 + 7 + beside)
    xe.start_rows()
    ce.start_rows()
    xe.start_slabs(False)
    ce.tail[...] = pack_tail(cv[:, 128:C])

    w1n[...] = jnp.zeros_like(w1n)
    w1t[...] = jnp.zeros_like(w1t)
    w2t[...] = jnp.zeros_like(w2t)
    gz[0:2 * ROW] = jnp.zeros((2 * ROW, CP), BF)
    gz[2 * ROW + CELLS:] = jnp.zeros((gz.shape[0] - 2 * ROW - CELLS, CP), BF)
    for e, v in ((xe, xv), (ce, cv)):
        e.ext[1, ROW:ROW + CELLS, 0:128] = v[:, :128]
        e.ext[1, ROW:ROW + CELLS, 128:256] = jnp.concatenate(
            [v[:, 128:C], jnp.zeros((CELLS, 64), BF)], axis=1)
    for w in (0, 1):
        part[w, 324:] = jnp.zeros((UNITS - 324, 8, 128), BF)
    for slot in range(3):
        xe.ext[slot, 2 * ROW + CELLS:] = jnp.zeros((EXT - 2 * ROW - CELLS, CP), BF)
    loads[2].wait()
    loads[3].wait()
    for b in range(3):
        for a in range(3):
            w1n[b, a * CP:a * CP + C, 0:C] = wv1[a * 3 + b]
            w1t[b, 0:C, a * CP:a * CP + C] = wv1[(2 - a) * 3 + 2 - b]
            w2t[b, 0:C, a * CP:a * CP + C] = wv2[(2 - a) * 3 + 2 - b]

    def taps(ext, slot, i):
        start = pl.multiple_of(i * BLK, BLK)
        return jnp.concatenate([ext[slot, pl.ds(start + a * ROW, BLK), :] for a in range(3)], axis=1)

    def straight(ext, slot, i, w):
        return jnp.dot(taps(ext, slot, i), w[slot], preferred_element_type=F32)

    def flipped(ext, slot, i, w):
        return lax.dot_general(taps(ext, slot, i), w[slot], (((1,), (1,)), ((), ())),
                               preferred_element_type=F32)

    def rows_of(i):
        return pl.ds(pl.multiple_of(i * BLK, BLK), BLK)

    def add_slab(acc, conv, ext, slot, w, new):
        @pl.loop(0, CELLS // BLK)
        def _(i):
            value = conv(ext, slot, i, w)
            acc[rows_of(i)] = value if new else acc[rows_of(i)] + value

    def put_tap(which, tap, grad):
        main = grad[:, :128].reshape(24, 8, 128)
        tail = jnp.concatenate([grad[:96, 128:C], grad[96:, 128:C]], axis=1).reshape(12, 8, 128)
        part[which, pl.ds(tap * TAPU, 24)] = main.astype(BF)
        part[which, pl.ds(tap * TAPU + 24, 12)] = tail.astype(BF)

    ce.start_slabs(False)
    xe.arrive_rows(2)
    ce.arrive_rows(2)
    xe.start_slabs(True)
    ce.start_slabs(True)
    add_slab(acc_x, straight, xe.ext, 1, w1n, True)
    x_t[1] = xe.ext[1].T

    def take_x(k):
        xe.arrive_rows(k)
        xe.arrive(k)
        add_slab(acc_x, straight, xe.ext, 2 * k, w1n, False)
        x_t[2 * k] = xe.ext[2 * k].T

    take_x(1 - core)
    add_slab(acc_c, flipped, ce.ext, 1, w2t, True)
    take_x(core)

    @pl.loop(0, CELLS // BLK)
    def _(i):
        pre = acc_x[rows_of(i)]
        sig = 1.0 / (1.0 + jnp.exp(-pre))
        hid_t[:, rows_of(i)] = (pre * sig).astype(BF).T
        acc_x[rows_of(i)] = sig * (1.0 + pre * (1.0 - sig))

    def second_grad(slot):
        @pl.loop(0, 3)
        def _(a):
            rhs = ce.ext[slot, pl.ds(pl.multiple_of((2 - a) * ROW, ROW), CELLS), :]
            put_tap(1, a * 3 + 2 - slot, jnp.dot(hid_t[0:C], rhs, preferred_element_type=F32))

    second_grad(1)
    for k in (0, 1):
        ce.arrive_rows(k)
        ce.arrive(k)
        add_slab(acc_c, flipped, ce.ext, 2 * k, w2t, False)

    @pl.loop(0, CELLS // BLK)
    def _(i):
        value = (acc_c[rows_of(i)] * acc_x[rows_of(i)]).astype(BF)
        gz[pl.ds(pl.multiple_of(i * BLK + 2 * ROW, 2 * ROW), BLK)] = value
        pe.ext[1, pl.ds(pl.multiple_of(i * BLK + ROW, ROW), BLK)] = value
    pe.fill_rows(gz[CELLS + ROW:CELLS + 2 * ROW], gz[2 * ROW:3 * ROW])
    pe.start_rows()
    pe.tail[...] = pack_tail(gz[2 * ROW:2 * ROW + CELLS, 128:C])
    pe.start_slabs(False)

    @pl.loop(0, 3)
    def _(a):
        rhs = gz[pl.ds(pl.multiple_of((2 - a) * ROW, ROW), EXT), :]
        for b in range(3):
            put_tap(0, a * 3 + b, jnp.dot(x_t[b, 0:C], rhs, preferred_element_type=F32))

    one, two = (Chain(w, part, ff, refs, core, pos1, pos2, z, partner, first, second, third)
                for w, refs in enumerate(chains))
    one.swap_start()
    second_grad(0)
    second_grad(2)
    two.swap_start()
    one.swap_end()
    pe.arrive_rows(2)
    add_slab(acc_x, flipped, pe.ext, 1, w1t, True)
    two.swap_end()

    def take_p(k, across):
        @pl.when(pe.comes_across(k) == across)
        def _():
            pe.arrive_rows(k)
            pe.arrive(k)
            add_slab(acc_x, flipped, pe.ext, 2 * k, w1t, False)

    take_p(0, False)
    one.first_end()
    take_p(1, False)
    two.first_end()
    one.second_end()
    two.second_end()
    pe.start_slabs(True)
    xe.drain()
    ce.drain()
    one.third_end()
    two.third_end()
    take_p(0, True)
    take_p(1, True)
    one.gather_second()
    two.gather_second()
    one.gather_first()
    two.gather_first()

    @pl.loop(0, CELLS // BLK)
    def _(i):
        dxv[rows_of(i)] = acc_x[rows_of(i), 0:C].astype(BF)
    dx_out = pltpu.make_async_copy(dxv, dx_ref, out_sem.at[0])
    dx_out.start()
    pe.drain()
    outs = []
    for chain in (one, two):
        chain.back_end()
        out = pltpu.make_async_copy(ff.at[chain.w], ff_ref.at[chain.w], out_sem.at[1 + chain.w])
        out.start()
        outs.append(out)
    for out in outs:
        out.wait()
    dx_out.wait()


def finish(scale, ff_ref, dx_ref, g1_ref, g2_ref, out_ref, ffv, gv, dxv, sem_in, sem_out):
    parts = [(j, which) for j in range(3) for which in (0, 1)]

    def take(j, which):
        units = pl.ds(j * 3 * TAPU, 3 * TAPU)
        return pltpu.make_async_copy(ff_ref.at[which, units], ffv.at[which, units], sem_in.at[which, j])

    def give(j, which):
        rows = pl.ds(j * 3 * C, 3 * C)
        return pltpu.make_async_copy(gv.at[which, rows], (g1_ref, g2_ref)[which].at[rows], sem_out.at[which, j])

    dx_in = pltpu.make_async_copy(dx_ref, dxv, sem_in.at[0, 3])
    dx_out = pltpu.make_async_copy(dxv, out_ref, sem_out.at[0, 3])
    for part in parts:
        take(*part).start()
    dx_in.start()
    for j, which in parts:
        take(j, which).wait()
        for t in range(3 * j, 3 * j + 3):
            main = ffv[which, t * TAPU:t * TAPU + 24].astype(F32).reshape(C, 128) * scale
            tail = ffv[which, t * TAPU + 24:(t + 1) * TAPU].astype(F32).reshape(96, 128) * scale
            row = t * C
            gv[which, row:row + C, 0:128] = main
            gv[which, row:row + 96, 128:C] = tail[:, :64]
            gv[which, row + 96:row + C, 128:C] = tail[:, 64:]
        give(j, which).start()
        if (j, which) == (0, 1):
            dx_in.wait()
            dx_out.start()
    for part in parts:
        give(*part).wait()
    dx_out.wait()


def shards(n_lon, n_lat, inputs, cotangent, first_weight, second_weight):
    height, width, channels = inputs.shape
    scale = 1.0 / math.sqrt(height * n_lat * width * n_lon)
    dma = pltpu.SemaphoreType.DMA
    scratch = exchange_scratch() * 3 + [
        pltpu.VMEM((CELLS, C), BF),
        pltpu.VMEM((CELLS, C), BF),
        pltpu.VMEM((9, C, C), BF),
        pltpu.VMEM((9, C, C), BF),
        dma((4,)),
        pltpu.VMEM((3, 3 * CP, CP), BF),
        pltpu.VMEM((3, CP, 3 * CP), BF),
        pltpu.VMEM((3, CP, 3 * CP), BF),
        pltpu.VMEM((CELLS, CP), F32),
        pltpu.VMEM((CELLS, CP), F32),
        pltpu.VMEM((CP, CELLS), BF),
        pltpu.VMEM((3, CP, EXT), BF),
        pltpu.VMEM((EXT + 2 * ROW, CP), BF),
        pltpu.VMEM((2, UNITS, 8, 128), BF),
        pltpu.VMEM((CELLS, C), BF),
        dma((3,)),
        pltpu.VMEM((2, UNITS, 8, 128), BF),
    ] + [
        pltpu.VMEM((HALF, 8, 128), BF),
        pltpu.VMEM((HALF, 8, 128), BF),
        pltpu.VMEM((8, 128), F32),
        pltpu.VMEM((3, QUART, 8, 128), BF),
        pltpu.VMEM((QUART, 8, 128), BF),
        pltpu.VMEM((QUART, 8, 128), F32),
        pltpu.VMEM((3, SIXTH, 8, 128), BF),
        pltpu.VMEM((8, SIXTH, 8, 128), BF),
        dma((2,)), dma((2, 3)), dma((2, 3)), dma((2, 7)), dma((2, 3)), dma((2, 3, 4)),
        dma((2, 4)), dma((1,)),
    ] * 2
    dx, ff = pl.pallas_call(
        functools.partial(kernel, n_lon, n_lat),
        out_shape=(jax.ShapeDtypeStruct((CELLS, C), BF),
                   jax.ShapeDtypeStruct((2, UNITS, 8, 128), BF)),
        in_specs=[pl.BlockSpec(memory_space=pl.ANY)] * 4,
        out_specs=(pl.BlockSpec(memory_space=pl.ANY),) * 2,
        scratch_shapes=scratch,
        compiler_params=pltpu.CompilerParams(collective_id=0, has_side_effects=True,
                                             vmem_limit_bytes=60 << 20),
        name="conv_grads",
    )(inputs.reshape(CELLS, C), cotangent.reshape(CELLS, C),
      first_weight.reshape(9, C, C), second_weight.reshape(9, C, C))
    anywhere = pl.BlockSpec(memory_space=pl.ANY)
    g1, g2, dx = pl.pallas_call(
        functools.partial(finish, scale),
        out_shape=(jax.ShapeDtypeStruct((9 * C, C), F32),) * 2 + (jax.ShapeDtypeStruct((CELLS, C), BF),),
        in_specs=[anywhere] * 2,
        out_specs=(anywhere,) * 3,
        scratch_shapes=[
            pltpu.VMEM((2, UNITS, 8, 128), BF),
            pltpu.VMEM((2, 9 * C, C), F32),
            pltpu.VMEM((CELLS, C), BF),
            dma((2, 4)),
            dma((2, 4)),
        ],
        compiler_params=pltpu.CompilerParams(vmem_limit_bytes=60 << 20),
        name="unpack_grads",
    )(ff, dx)
    return (dx.reshape(height, width, channels), g1.reshape(3, 3, C, C), g2.reshape(3, 3, C, C))


def solution(mesh):
    placed = (P("lat", "lon", None), P("lat", "lon", None), P(), P())
    return jax.shard_map(
        functools.partial(shards, mesh.shape["lon"], mesh.shape["lat"]),
        mesh=mesh,
        in_specs=placed,
        out_specs=(P("lat", "lon", None), P(), P()),
        check_vma=False,
    )
```

time: 86.3 us -> 71.6 us (0.83)
  Pallas kernels: 83.6 us -> 70.8 us
  local copies, waits for them, and re-layouts: 1.87 us -> 0 us
    pallas_call x1, Pallas kernels: 78.9 us -> 67.5 us  [shards(): pl.pallas_call(functools.partial(kernel, n_lon, n_lat), out_shape=(jax.Sh...]
    unnamed x1 -> x0, local copies, waits for them, and re-layouts: 1.87 us -> none
    pallas_call x1, Pallas kernels: 4.62 us -> 3.29 us  [shards(): pl.pallas_call(functools.partial(finish, scale), out_shape=(jax.ShapeDtyp...]
where the time goes in v2:
time: 71.6 us; the launch traced here: 71.4 us
  Pallas kernels  70.8 us (99%)
    pallas_call x1, Pallas kernels, shards(): pl.pallas_call(functools.partial(kernel, n_lon, n_lat), out_shape=(jax.Sh...  67.5 us
    pallas_call x1, Pallas kernels, shards(): pl.pallas_call(functools.partial(finish, scale), out_shape=(jax.ShapeDtyp...  3.29 us

profile of v2, /device:TPU:1, one launch (start us, length us, event | category | flops | bytes accessed | tf_op | source)
XLA Modules:
  0.0 71.4 jit_solution(13833089932720457941)
XLA Ops:
  0.6 67.5 %conv_grads.1 = (bf16[1024,192]{1,0:T(8,128)(2,1)}, bf16[2,352,8,128]{3,2,1,0:T(8,128)(2,1)}) custom-call(bf16[1024,192]{1,0:T(8,128)(2,1)} %bitcast.9, bf16[1024,192]{1,0:T(8,128)(2,1)} %bitcast.10, bf16[9,192,192]{2,1,0:T(8,128)(2,1)} %bitcast.7, bf16[9,192,192]{2,1,0:T(8,128)(2,1)} %bitcast.8), custom_call_target="tpu_custom_call" | custom-call | tf_op jit(solution)/shard_map/conv_grads/pallas_call | solution.py:542
  68.1 3.3 %unpack_grads.1 = (f32[1728,192]{1,0:T(8,128)}, f32[1728,192]{1,0:T(8,128)}, bf16[1024,192]{1,0:T(8,128)(2,1)}) custom-call(bf16[2,352,8,128]{3,2,1,0:T(8,128)(2,1)} %get-tuple-element.8.ff_ref, bf16[1024,192]{1,0:T(8,128)(2,1)} %get-tuple-element.9.dx_ref), custom_call_target="tpu_custom_call" | custom-call | tf_op jit(solution)/shard_map/unpack_grads/pallas_call | solution.py:555

commit v3 on v2

--- a/solution.py
+++ b/solution.py
@@ -65,10 +65,19 @@
     def tail_copy(self, k):
         return self.copy(self.tail, self.tail_in.at[k], 2 + k, self.target(k), self.lat)
 
-    def row_copy(self, k, side):
+    def row_copy(self, side):
         lat = jnp.minimum(self.lat + 1, self.n_lat - 1) if side == 0 else jnp.maximum(self.lat - 1, 0)
-        return self.copy(self.rows.at[side], self.rows_in.at[2 * k + side],
-                         4 + 2 * k + side, self.target(k), lat)
+        return self.copy(self.rows.at[side], self.rows_in.at[4 + side], 4 + side, self.lon, lat)
+
+    def pass_copy(self, k, side):
+        return self.copy(self.rows_in.at[4 + side], self.rows_in.at[2 * k + side],
+                         6 + 2 * k + side, self.target(k), self.lat)
+
+    def has_row(self, side):
+        return self.lat > 0 if side == 0 else self.lat < self.n_lat - 1
+
+    def sends_row(self, side):
+        return self.has_row(1 - side)
 
     def start_slabs(self, across):
         for k in (0, 1):
@@ -83,29 +92,39 @@
             self.rows[side, ROW:] = pack_tail(part[:, 128:C])
 
     def start_rows(self):
-        for k in range(3):
-            @pl.when(self.lat < self.n_lat - 1)
-            def _():
-                self.row_copy(k, 0).start()
-
-            @pl.when(self.lat > 0)
-            def _():
-                self.row_copy(k, 1).start()
-
-    def arrive_rows(self, k):
-        slot = 1 if isinstance(k, int) and k == 2 else 2 * k
+        for side in (0, 1):
+            @pl.when(self.sends_row(side))
+            def _():
+                self.row_copy(side).start()
+
+    def own_rows(self):
+        for side in (0, 1):
+            @pl.when(self.has_row(side))
+            def _():
+                self.row_copy(side).wait_recv()
+                for k in (0, 1):
+                    self.pass_copy(k, side).start()
+        self.place_rows(2, 1)
+
+    def place_rows(self, k, slot):
         zero = jnp.zeros((ROW, CP), BF)
-        for side, start, here in ((0, 0, self.lat > 0), (1, ROW + CELLS, self.lat < self.n_lat - 1)):
-            @pl.when(here)
-            def _():
-                self.row_copy(k, side).wait_recv()
+        for side, start in ((0, 0), (1, ROW + CELLS)):
+            @pl.when(self.has_row(side))
+            def _():
                 packed = self.rows_in[2 * k + side]
                 self.ext[slot, start:start + ROW, 0:128] = packed[:ROW]
                 unpack_tail(self.ext, slot, start, packed[ROW:])
 
-            @pl.when(jnp.logical_not(here))
+            @pl.when(jnp.logical_not(self.has_row(side)))
             def _():
                 self.ext[slot, start:start + ROW] = zero
+
+    def arrive_rows(self, k):
+        for side in (0, 1):
+            @pl.when(self.has_row(side))
+            def _():
+                self.pass_copy(k, side).wait_recv()
+        self.place_rows(k, 2 * k)
 
     def arrive(self, k):
         self.tail_copy(k).wait_recv()
@@ -116,14 +135,15 @@
         for k in (0, 1):
             self.main_copy(k).wait_send()
             self.tail_copy(k).wait_send()
-        for k in range(3):
-            @pl.when(self.lat < self.n_lat - 1)
-            def _():
-                self.row_copy(k, 0).wait_send()
-
-            @pl.when(self.lat > 0)
-            def _():
-                self.row_copy(k, 1).wait_send()
+        for side in (0, 1):
+            @pl.when(self.sends_row(side))
+            def _():
+                self.row_copy(side).wait_send()
+
+            @pl.when(self.has_row(side))
+            def _():
+                for k in (0, 1):
+                    self.pass_copy(k, side).wait_send()
 
 
 def exchange_scratch():
@@ -147,11 +167,11 @@
 
 
 class Chain:
-    def __init__(self, w, part, ff, refs, core, pos1, pos2, z, partner, first, second, third):
-        self.w, self.part, self.ff = w, part, ff
+    def __init__(self, w, part, ff, out, refs, core, pos1, pos2, z, partner, first, second, third):
+        self.w, self.part, self.ff, self.out = w, part, ff, out
         (self.pair_in, self.s0, self.own0, self.r1, self.s1, self.own1, self.r2, self.r3,
          self.pair, self.sem1, self.sem2, self.sem3, self.sem4, self.sem5,
-         self.sem6, self.spare) = refs
+         self.sem6, self.sem7) = refs
         self.core, self.pos1, self.pos2, self.z = core, pos1, pos2, z
         self.partner, self.first, self.second, self.third = partner, first, second, third
 
@@ -184,8 +204,13 @@
 
     def back(self, k, theirs=False):
         core = 1 - self.core if theirs else self.core
-        spot = self.ff.at[self.w, pl.ds(core * HALF + lax.rem(self.pos1 + 4 - k, 4) * QUART, QUART)]
-        return remote(spot, spot, self.sem6.at[0, k], self.sem6.at[1, k], self.partner)
+        spot = pl.ds(core * HALF + lax.rem(self.pos1 + 4 - k, 4) * QUART, QUART)
+        return remote(self.ff.at[self.w, spot], self.out.at[self.w, spot],
+                      self.sem6.at[0, k], self.sem6.at[1, k], self.partner)
+
+    def keep(self, k):
+        spot = pl.ds(self.core * HALF + lax.rem(self.pos1 + 4 - k, 4) * QUART, QUART)
+        return pltpu.make_async_copy(self.ff.at[self.w, spot], self.out.at[self.w, spot], self.sem7.at[k])
 
     def swap_start(self):
         self.swap().start()
@@ -237,16 +262,19 @@
             for k in (1, 2, 3):
                 self.spread(k, j).start()
         self.back(0).start()
+        self.keep(0).start()
 
     def gather_first(self):
         for k in (1, 2, 3):
             for j in range(4):
                 self.spread(k, j, 4 - k).wait_recv()
             self.back(k).start()
+            self.keep(k).start()
 
     def back_end(self):
         for k in range(4):
             self.back(k, True).wait_recv()
+            self.keep(k).wait()
         for k in range(4):
             self.back(k).wait_send()
         for k in (1, 2, 3):
@@ -292,8 +320,7 @@
     for da, here in ((-1, lat > 0), (1, lat < n_lat - 1)):
         @pl.when(here)
         def _():
-            for dl in (-2, -1, 0, 1, 2):
-                greet({"lon": lax.rem(lon + n_lon + dl, n_lon), "lat": lat + da})
+            greet({"lon": lon, "lat": lat + da})
     for k in (1, 2, 3):
         greet(first(k))
         greet(second(k))
@@ -311,7 +338,7 @@
         load.wait()
         e.fill_rows(v[CELLS - ROW:], v[:ROW])
     xe.tail[...] = pack_tail(xv[:, 128:C])
-    beside = jnp.where(lat > 0, 5, 0) + jnp.where(lat < n_lat - 1, 5, 0)
+    beside = jnp.where(lat > 0, 1, 0) + jnp.where(lat < n_lat - 1, 1, 0)
     pl.semaphore_wait(barrier, 4 + 6 + 7 + beside)
     xe.start_rows()
     ce.start_rows()
@@ -365,10 +392,10 @@
         part[which, pl.ds(tap * TAPU, 24)] = main.astype(BF)
         part[which, pl.ds(tap * TAPU + 24, 12)] = tail.astype(BF)
 
+    xe.own_rows()
+    ce.own_rows()
+    xe.start_slabs(True)
     ce.start_slabs(False)
-    xe.arrive_rows(2)
-    ce.arrive_rows(2)
-    xe.start_slabs(True)
     ce.start_slabs(True)
     add_slab(acc_x, straight, xe.ext, 1, w1n, True)
     x_t[1] = xe.ext[1].T
@@ -397,7 +424,8 @@
             put_tap(1, a * 3 + 2 - slot, jnp.dot(hid_t[0:C], rhs, preferred_element_type=F32))
 
     second_grad(1)
-    for k in (0, 1):
+    late = jnp.where(ce.comes_across(0), 0, 1)
+    for k in (1 - late, late):
         ce.arrive_rows(k)
         ce.arrive(k)
         add_slab(acc_c, flipped, ce.ext, 2 * k, w2t, False)
@@ -418,14 +446,14 @@
         for b in range(3):
             put_tap(0, a * 3 + b, jnp.dot(x_t[b, 0:C], rhs, preferred_element_type=F32))
 
-    one, two = (Chain(w, part, ff, refs, core, pos1, pos2, z, partner, first, second, third)
+    one, two = (Chain(w, part, ff, ff_ref, refs, core, pos1, pos2, z, partner, first, second, third)
                 for w, refs in enumerate(chains))
     one.swap_start()
     second_grad(0)
     second_grad(2)
     two.swap_start()
     one.swap_end()
-    pe.arrive_rows(2)
+    pe.own_rows()
     add_slab(acc_x, flipped, pe.ext, 1, w1t, True)
     two.swap_end()
 
@@ -447,10 +475,10 @@
     ce.drain()
     one.third_end()
     two.third_end()
+    one.gather_second()
+    two.gather_second()
     take_p(0, True)
     take_p(1, True)
-    one.gather_second()
-    two.gather_second()
     one.gather_first()
     two.gather_first()
 
@@ -460,48 +488,31 @@
     dx_out = pltpu.make_async_copy(dxv, dx_ref, out_sem.at[0])
     dx_out.start()
     pe.drain()
-    outs = []
     for chain in (one, two):
         chain.back_end()
-        out = pltpu.make_async_copy(ff.at[chain.w], ff_ref.at[chain.w], out_sem.at[1 + chain.w])
-        out.start()
-        outs.append(out)
-    for out in outs:
-        out.wait()
     dx_out.wait()
 
 
-def finish(scale, ff_ref, dx_ref, g1_ref, g2_ref, out_ref, ffv, gv, dxv, sem_in, sem_out):
-    parts = [(j, which) for j in range(3) for which in (0, 1)]
-
-    def take(j, which):
-        units = pl.ds(j * 3 * TAPU, 3 * TAPU)
-        return pltpu.make_async_copy(ff_ref.at[which, units], ffv.at[which, units], sem_in.at[which, j])
-
-    def give(j, which):
-        rows = pl.ds(j * 3 * C, 3 * C)
-        return pltpu.make_async_copy(gv.at[which, rows], (g1_ref, g2_ref)[which].at[rows], sem_out.at[which, j])
-
-    dx_in = pltpu.make_async_copy(dx_ref, dxv, sem_in.at[0, 3])
-    dx_out = pltpu.make_async_copy(dxv, out_ref, sem_out.at[0, 3])
-    for part in parts:
-        take(*part).start()
-    dx_in.start()
-    for j, which in parts:
-        take(j, which).wait()
-        for t in range(3 * j, 3 * j + 3):
-            main = ffv[which, t * TAPU:t * TAPU + 24].astype(F32).reshape(C, 128) * scale
-            tail = ffv[which, t * TAPU + 24:(t + 1) * TAPU].astype(F32).reshape(96, 128) * scale
-            row = t * C
+def finish(scale, ffv, dxv, g1_ref, g2_ref, out_ref, gv, sem_out):
+    taps = [(t, which) for t in (0, 3, 6) for which in (0, 1)]
+
+    def give(t, which):
+        rows = pl.ds(t * C, 3 * C)
+        return pltpu.make_async_copy(gv.at[which, rows], (g1_ref, g2_ref)[which].at[rows], sem_out.at[which, t])
+
+    dx_out = pltpu.make_async_copy(dxv, out_ref, sem_out.at[0, 9])
+    dx_out.start()
+    for t, which in taps:
+        for u in range(t, t + 3):
+            main = ffv[which, u * TAPU:u * TAPU + 24].astype(F32).reshape(C, 128) * scale
+            tail = ffv[which, u * TAPU + 24:(u + 1) * TAPU].astype(F32).reshape(96, 128) * scale
+            row = u * C
             gv[which, row:row + C, 0:128] = main
             gv[which, row:row + 96, 128:C] = tail[:, :64]
             gv[which, row + 96:row + C, 128:C] = tail[:, 64:]
-        give(j, which).start()
-        if (j, which) == (0, 1):
-            dx_in.wait()
-            dx_out.start()
-    for part in parts:
-        give(*part).wait()
+        give(t, which).start()
+    for tap in taps:
+        give(*tap).wait()
     dx_out.wait()
 
 
@@ -525,7 +536,7 @@
         pltpu.VMEM((EXT + 2 * ROW, CP), BF),
         pltpu.VMEM((2, UNITS, 8, 128), BF),
         pltpu.VMEM((CELLS, C), BF),
-        dma((3,)),
+        dma((1,)),
         pltpu.VMEM((2, UNITS, 8, 128), BF),
     ] + [
         pltpu.VMEM((HALF, 8, 128), BF),
@@ -537,34 +548,32 @@
         pltpu.VMEM((3, SIXTH, 8, 128), BF),
         pltpu.VMEM((8, SIXTH, 8, 128), BF),
         dma((2,)), dma((2, 3)), dma((2, 3)), dma((2, 7)), dma((2, 3)), dma((2, 3, 4)),
-        dma((2, 4)), dma((1,)),
+        dma((2, 4)), dma((4,)),
     ] * 2
     dx, ff = pl.pallas_call(
         functools.partial(kernel, n_lon, n_lat),
         out_shape=(jax.ShapeDtypeStruct((CELLS, C), BF),
                    jax.ShapeDtypeStruct((2, UNITS, 8, 128), BF)),
-        in_specs=[pl.BlockSpec(memory_space=pl.ANY)] * 4,
+        in_specs=[pl.BlockSpec(memory_space=pltpu.MemorySpace.HBM)] * 4,
         out_specs=(pl.BlockSpec(memory_space=pl.ANY),) * 2,
         scratch_shapes=scratch,
         compiler_params=pltpu.CompilerParams(collective_id=0, has_side_effects=True,
-                                             vmem_limit_bytes=60 << 20),
+                                             vmem_limit_bytes=32 << 20),
         name="conv_grads",
-    )(inputs.reshape(CELLS, C), cotangent.reshape(CELLS, C),
-      first_weight.reshape(9, C, C), second_weight.reshape(9, C, C))
+    )(*(pltpu.with_memory_space_constraint(v, pltpu.MemorySpace.HBM) for v in (
+        inputs.reshape(CELLS, C), cotangent.reshape(CELLS, C),
+        first_weight.reshape(9, C, C), second_weight.reshape(9, C, C))))
     anywhere = pl.BlockSpec(memory_space=pl.ANY)
     g1, g2, dx = pl.pallas_call(
         functools.partial(finish, scale),
         out_shape=(jax.ShapeDtypeStruct((9 * C, C), F32),) * 2 + (jax.ShapeDtypeStruct((CELLS, C), BF),),
-        in_specs=[anywhere] * 2,
+        in_specs=[pl.BlockSpec(memory_space=pltpu.VMEM)] * 2,
         out_specs=(anywhere,) * 3,
         scratch_shapes=[
-            pltpu.VMEM((2, UNITS, 8, 128), BF),
             pltpu.VMEM((2, 9 * C, C), F32),
-            pltpu.VMEM((CELLS, C), BF),
-            dma((2, 4)),
-            dma((2, 4)),
+            dma((2, 10)),
         ],
-        compiler_params=pltpu.CompilerParams(vmem_limit_bytes=60 << 20),
+        compiler_params=pltpu.CompilerParams(vmem_limit_bytes=24 << 20),
         name="unpack_grads",
     )(ff, dx)
     return (dx.reshape(height, width, channels), g1.reshape(3, 3, C, C), g2.reshape(3, 3, C, C))

time: 71.6 us -> 69 us (0.964)
  Pallas kernels: 70.8 us -> 68.3 us
    pallas_call x1, Pallas kernels: 67.5 us -> 66.2 us  [shards(): pl.pallas_call(functools.partial(kernel, n_lon, n_lat), out_shape=(jax.Sh...]
    pallas_call x1, Pallas kernels: 3.29 us -> 2.14 us  [shards(): pl.pallas_call(functools.partial(finish, scale), out_shape=(jax.ShapeDtyp...]
where the time goes in v3:
time: 69 us; the launch traced here: 68.9 us
  Pallas kernels  68.3 us (99%)
    pallas_call x1, Pallas kernels, shards(): pl.pallas_call(functools.partial(kernel, n_lon, n_lat), out_shape=(jax.Sh...  66.2 us
    pallas_call x1, Pallas kernels, shards(): pl.pallas_call(functools.partial(finish, scale), out_shape=(jax.ShapeDtyp...  2.14 us

profile of v3, /device:TPU:1, one launch (start us, length us, event | category | flops | bytes accessed | tf_op | source)
XLA Modules:
  0.0 68.9 jit_solution(15222320948594231677)
XLA Ops:
  0.6 66.2 %conv_grads.1 = (bf16[1024,192]{1,0:T(8,128)(2,1)S(1)}, bf16[2,352,8,128]{3,2,1,0:T(8,128)(2,1)S(1)}) custom-call(bf16[1024,192]{1,0:T(8,128)(2,1)} %bitcast.9, bf16[1024,192]{1,0:T(8,128)(2,1)} %bitcast.10, bf16[9,192,192]{2,1,0:T(8,128)(2,1)} %bitcast.7, bf16[9,192,192]{2,1,0:T(8,128)(2,1)} %bitcast.8), custom_call_target="tpu_custom_call" | custom-call | tf_op jit(solution)/shard_map/conv_grads/pallas_call | solution.py:553
  66.8 2.1 %unpack_grads.1 = (f32[1728,192]{1,0:T(8,128)}, f32[1728,192]{1,0:T(8,128)}, bf16[1024,192]{1,0:T(8,128)(2,1)}) custom-call(bf16[2,352,8,128]{3,2,1,0:T(8,128)(2,1)S(1)} %get-tuple-element.8.ffv, bf16[1024,192]{1,0:T(8,128)(2,1)S(1)} %get-tuple-element.9.dxv), custom_call_target="tpu_custom_call" | custom-call | tf_op jit(solution)/shard_map/unpack_grads/pallas_call | solution.py:567

commit v4 on v3

--- a/solution.py
+++ b/solution.py
@@ -48,7 +48,7 @@
 
     def crosses(self, k):
         place = lax.rem(self.lon, 16)
-        return place >= 16 - self.dist if k == 0 else place < self.dist
+        return jnp.where(k == 0, place >= 16 - self.dist, place < self.dist)
 
     def comes_across(self, k):
         return self.crosses(1 - k)
@@ -97,14 +97,18 @@
             def _():
                 self.row_copy(side).start()
 
-    def own_rows(self):
+    def take_rows(self):
         for side in (0, 1):
             @pl.when(self.has_row(side))
             def _():
                 self.row_copy(side).wait_recv()
+
+    def pass_rows(self):
+        for side in (0, 1):
+            @pl.when(self.has_row(side))
+            def _():
                 for k in (0, 1):
                     self.pass_copy(k, side).start()
-        self.place_rows(2, 1)
 
     def place_rows(self, k, slot):
         zero = jnp.zeros((ROW, CP), BF)
@@ -219,7 +223,7 @@
         self.swap().wait()
         mine = self.part[self.w, pl.ds(self.core * HALF, HALF)].astype(F32) + self.pair_in[...].astype(F32)
         self.s0[...] = mine.astype(BF)
-        for k in (1, 2, 3):
+        for k in (2, 1, 3):
             self.to_first(k).start()
 
     def first_end(self):
@@ -231,7 +235,7 @@
             total += self.r1[k - 1].astype(F32)
         self.own1[...] = total
         self.s1[...] = total.astype(BF)
-        for k in (1, 2, 3):
+        for k in (2, 1, 3):
             self.to_second(k).start()
 
     def second_end(self):
@@ -240,7 +244,7 @@
             self.to_second(k).wait()
             total += self.r2[k - 1].astype(F32)
         self.r3[self.z] = total.astype(BF)
-        for k in range(1, 8):
+        for k in (4, 3, 5, 2, 6, 1, 7):
             self.to_third(k).start()
 
     def third_end(self):
@@ -251,21 +255,21 @@
         for k in range(1, 8):
             total += self.r3[k].astype(F32)
         self.ff[self.w, pl.ds(self.core * HALF + self.pos1 * QUART + self.pos2 * SIXTH, SIXTH)] = total.astype(BF)
-        for k in (1, 2, 3):
+        for k in (2, 1, 3):
             self.piece(k).start()
-        for k in (1, 2, 3):
+        for k in (2, 1, 3):
             self.spread(k, 0).start()
 
     def gather_second(self):
-        for j in (1, 2, 3):
+        for j in (1, 3, 2):
             self.piece(j, 4 - j).wait_recv()
-            for k in (1, 2, 3):
+            for k in (2, 1, 3):
                 self.spread(k, j).start()
         self.back(0).start()
         self.keep(0).start()
 
     def gather_first(self):
-        for k in (1, 2, 3):
+        for k in (1, 3, 2):
             for j in range(4):
                 self.spread(k, j, 4 - k).wait_recv()
             self.back(k).start()
@@ -310,6 +314,10 @@
     pos1 = x * (1 - core) + y * core
     pos2 = y * (1 - core) + x * core
 
+    loads = [pltpu.make_async_copy(src, dst, load_sem.at[i]) for i, (src, dst) in enumerate(
+        ((x_ref, xv), (c_ref, cv), (w1_ref, wv1), (w2_ref, wv2)))]
+    for load in loads:
+        load.start()
     barrier = pltpu.get_barrier_semaphore()
 
     def greet(dev):
@@ -330,18 +338,14 @@
     xe = Exchange(xb, x_ref.at[:, pl.ds(0, 128)], 1, lon, lat, n_lon, n_lat)
     ce = Exchange(cb, c_ref.at[:, pl.ds(0, 128)], 2, lon, lat, n_lon, n_lat)
     pe = Exchange(pb, gz.at[pl.ds(2 * ROW, CELLS), pl.ds(0, 128)], 1, lon, lat, n_lon, n_lat)
-    loads = [pltpu.make_async_copy(src, dst, load_sem.at[i]) for i, (src, dst) in enumerate(
-        ((x_ref, xv), (c_ref, cv), (w1_ref, wv1), (w2_ref, wv2)))]
-    for load in loads:
-        load.start()
     for e, v, load in ((xe, xv, loads[0]), (ce, cv, loads[1])):
         load.wait()
         e.fill_rows(v[CELLS - ROW:], v[:ROW])
-    xe.tail[...] = pack_tail(xv[:, 128:C])
     beside = jnp.where(lat > 0, 1, 0) + jnp.where(lat < n_lat - 1, 1, 0)
     pl.semaphore_wait(barrier, 4 + 6 + 7 + beside)
     xe.start_rows()
     ce.start_rows()
+    xe.tail[...] = pack_tail(xv[:, 128:C])
     xe.start_slabs(False)
     ce.tail[...] = pack_tail(cv[:, 128:C])
 
@@ -392,11 +396,15 @@
         part[which, pl.ds(tap * TAPU, 24)] = main.astype(BF)
         part[which, pl.ds(tap * TAPU + 24, 12)] = tail.astype(BF)
 
-    xe.own_rows()
-    ce.own_rows()
+    xe.take_rows()
+    ce.take_rows()
     xe.start_slabs(True)
+    xe.pass_rows()
+    ce.pass_rows()
     ce.start_slabs(False)
     ce.start_slabs(True)
+    xe.place_rows(2, 1)
+    ce.place_rows(2, 1)
     add_slab(acc_x, straight, xe.ext, 1, w1n, True)
     x_t[1] = xe.ext[1].T
 
@@ -438,6 +446,7 @@
     pe.fill_rows(gz[CELLS + ROW:CELLS + 2 * ROW], gz[2 * ROW:3 * ROW])
     pe.start_rows()
     pe.tail[...] = pack_tail(gz[2 * ROW:2 * ROW + CELLS, 128:C])
+    pe.start_slabs(True)
     pe.start_slabs(False)
 
     @pl.loop(0, 3)
@@ -453,32 +462,29 @@
     second_grad(2)
     two.swap_start()
     one.swap_end()
-    pe.own_rows()
+    pe.take_rows()
+    pe.pass_rows()
+    pe.place_rows(2, 1)
     add_slab(acc_x, flipped, pe.ext, 1, w1t, True)
     two.swap_end()
 
-    def take_p(k, across):
-        @pl.when(pe.comes_across(k) == across)
-        def _():
-            pe.arrive_rows(k)
-            pe.arrive(k)
-            add_slab(acc_x, flipped, pe.ext, 2 * k, w1t, False)
-
-    take_p(0, False)
+    def take_p(k):
+        pe.arrive_rows(k)
+        pe.arrive(k)
+        add_slab(acc_x, flipped, pe.ext, 2 * k, w1t, False)
+
+    take_p(1 - core)
     one.first_end()
-    take_p(1, False)
+    take_p(core)
     two.first_end()
     one.second_end()
     two.second_end()
-    pe.start_slabs(True)
     xe.drain()
     ce.drain()
     one.third_end()
     two.third_end()
     one.gather_second()
     two.gather_second()
-    take_p(0, True)
-    take_p(1, True)
     one.gather_first()
     two.gather_first()
 

time: 69 us -> 65.9 us (0.955)
  Pallas kernels: 68.3 us -> 65.1 us
    pallas_call x1, Pallas kernels: 66.2 us -> 63 us  [shards(): pl.pallas_call(functools.partial(kernel, n_lon, n_lat), out_shape=(jax.Sh...]
where the time goes in v4:
time: 65.9 us; the launch traced here: 65.8 us
  Pallas kernels  65.1 us (99%)
    pallas_call x1, Pallas kernels, shards(): pl.pallas_call(functools.partial(kernel, n_lon, n_lat), out_shape=(jax.Sh...  63 us
    pallas_call x1, Pallas kernels, shards(): pl.pallas_call(functools.partial(finish, scale), out_shape=(jax.ShapeDtyp...  2.14 us

profile of v4, /device:TPU:1, one launch (start us, length us, event | category | flops | bytes accessed | tf_op | source)
XLA Modules:
  0.0 65.8 jit_solution(11835444666878790678)
XLA Ops:
  0.6 63.0 %conv_grads.1 = (bf16[1024,192]{1,0:T(8,128)(2,1)S(1)}, bf16[2,352,8,128]{3,2,1,0:T(8,128)(2,1)S(1)}) custom-call(bf16[1024,192]{1,0:T(8,128)(2,1)} %bitcast.9, bf16[1024,192]{1,0:T(8,128)(2,1)} %bitcast.10, bf16[9,192,192]{2,1,0:T(8,128)(2,1)} %bitcast.7, bf16[9,192,192]{2,1,0:T(8,128)(2,1)} %bitcast.8), custom_call_target="tpu_custom_call" | custom-call | tf_op jit(solution)/shard_map/conv_grads/pallas_call | solution.py:559
  63.6 2.1 %unpack_grads.1 = (f32[1728,192]{1,0:T(8,128)}, f32[1728,192]{1,0:T(8,128)}, bf16[1024,192]{1,0:T(8,128)(2,1)}) custom-call(bf16[2,352,8,128]{3,2,1,0:T(8,128)(2,1)S(1)} %get-tuple-element.8.ffv, bf16[1024,192]{1,0:T(8,128)(2,1)S(1)} %get-tuple-element.9.dxv), custom_call_target="tpu_custom_call" | custom-call | tf_op jit(solution)/shard_map/unpack_grads/pallas_call | solution.py:573

commit v5 on v4

--- a/solution.py
+++ b/solution.py
@@ -79,8 +79,8 @@
     def sends_row(self, side):
         return self.has_row(1 - side)
 
-    def start_slabs(self, across):
-        for k in (0, 1):
+    def start_slabs(self, across, ks=(0, 1)):
+        for k in ks:
             @pl.when(self.crosses(k) == across)
             def _():
                 self.tail_copy(k).start()
@@ -347,6 +347,7 @@
     ce.start_rows()
     xe.tail[...] = pack_tail(xv[:, 128:C])
     xe.start_slabs(False)
+    xe.start_slabs(True, (1,))
     ce.tail[...] = pack_tail(cv[:, 128:C])
 
     w1n[...] = jnp.zeros_like(w1n)
@@ -398,7 +399,7 @@
 
     xe.take_rows()
     ce.take_rows()
-    xe.start_slabs(True)
+    xe.start_slabs(True, (0,))
     xe.pass_rows()
     ce.pass_rows()
     ce.start_slabs(False)
@@ -462,11 +463,11 @@
     second_grad(2)
     two.swap_start()
     one.swap_end()
+    two.swap_end()
     pe.take_rows()
     pe.pass_rows()
     pe.place_rows(2, 1)
     add_slab(acc_x, flipped, pe.ext, 1, w1t, True)
-    two.swap_end()
 
     def take_p(k):
         pe.arrive_rows(k)

time: 65.9 us -> 65.2 us (0.989)
  no operation moved by 1% of the time
where the time goes in v5:
time: 65.2 us; the launch traced here: 65.1 us
  Pallas kernels  64.5 us (99%)
    pallas_call x1, Pallas kernels, shards(): pl.pallas_call(functools.partial(kernel, n_lon, n_lat), out_shape=(jax.Sh...  62.4 us
    pallas_call x1, Pallas kernels, shards(): pl.pallas_call(functools.partial(finish, scale), out_shape=(jax.ShapeDtyp...  2.14 us

profile of v5, /device:TPU:1, one launch (start us, length us, event | category | flops | bytes accessed | tf_op | source)
XLA Modules:
  0.0 65.1 jit_solution(11066007071973898463)
XLA Ops:
  0.6 62.4 %conv_grads.1 = (bf16[1024,192]{1,0:T(8,128)(2,1)S(1)}, bf16[2,352,8,128]{3,2,1,0:T(8,128)(2,1)S(1)}) custom-call(bf16[1024,192]{1,0:T(8,128)(2,1)} %bitcast.9, bf16[1024,192]{1,0:T(8,128)(2,1)} %bitcast.10, bf16[9,192,192]{2,1,0:T(8,128)(2,1)} %bitcast.7, bf16[9,192,192]{2,1,0:T(8,128)(2,1)} %bitcast.8), custom_call_target="tpu_custom_call" | custom-call | tf_op jit(solution)/shard_map/conv_grads/pallas_call | solution.py:560
  63.0 2.1 %unpack_grads.1 = (f32[1728,192]{1,0:T(8,128)}, f32[1728,192]{1,0:T(8,128)}, bf16[1024,192]{1,0:T(8,128)(2,1)}) custom-call(bf16[2,352,8,128]{3,2,1,0:T(8,128)(2,1)S(1)} %get-tuple-element.8.ffv, bf16[1024,192]{1,0:T(8,128)(2,1)S(1)} %get-tuple-element.9.dxv), custom_call_target="tpu_custom_call" | custom-call | tf_op jit(solution)/shard_map/unpack_grads/pallas_call | solution.py:574
